TPU v7x, 32 devices: a whole 2x2x4 slice. The times are simulated.
32 devices in a mesh: groups: 2 (over y), tx: 4 (over z), ty: 4 (over x, core).
Axes of the slice: x: 2, y: 2, z: 4, core: 2. Of those that a mesh axis runs over, the one named last changes fastest.
Arguments:
- object_field: float32 [4, 256, 512], P('groups', 'tx', 'ty'), parts along dimension 0, may hold values from -4 to 4
- probe_modes: float32 [4, 8, 128, 128], P('groups'), parts along dimension 0, may hold values from -3 to 3
- positions: int32 [192, 2], P(('groups', 'tx', 'ty')), parts along dimension 0, may hold values from 0 to 384, as said below
- counts: int32 [32], P(('groups', 'tx', 'ty')), parts along dimension 0, may hold values from 1 to 6, as said below
- intensity: float32 [192, 128, 128], P(('groups', 'tx', 'ty')), parts along dimension 0, may hold values from 0.5 to 20
Outputs:
- object_out: float32 [4, 256, 512], P('groups', 'tx', 'ty'), parts along dimension 0
- probe_out: float32 [4, 8, 128, 128], P('groups'), parts along dimension 0
There are 2 independent parts, one for each index of `groups`. A program takes and returns all parts, laid end to end along the dimension named above; each array names one. Nothing has to cross between parts.
Inputs may be any that keep to these rules, and one draw needn't show every extreme that they name: `positions`: slot s belongs to tile t = s // 6, which covers object rows from (t // 4) * 64 on (64 rows) and columns from (t % 4) * 128 on (128 columns). The window of slot s, rows row to row + 127 and columns col to col + 127, lies inside the object and inside its tile widened by 64 pixels on every side. Tile t's live slots are its first counts[t] slots; the other slots are unused and their positions and intensity carry no meaning. Some tile has all 6 slots live.
All inputs are finite; a program needn't handle non-finite values.
Results may differ from a plain program's by a relative error of at most 0.0001.
Values sent between devices are 32-bit elements; how exact they have to be, the bound alone decides.
A program may use at most 64 MiB of HBM per device.

v0:
```python
import jax
import jax.numpy as jnp
import ml_dtypes
import numpy as np
from jax import lax
from jax.experimental import pallas as pl
from jax.experimental.pallas import tpu as pltpu
from jax.sharding import PartitionSpec as P

ITERS = 2


def with_halo(value, sides, width):
    for axis, dim in sides:
        size, length = (lax.axis_size(axis), value.shape[dim])
        up = [(i, (i + 1) % size) for i in range(size - 1)]
        down = [(j, i) for i, j in up]
        last = lax.slice_in_dim(value, length - width, length, axis=dim)
        first = lax.slice_in_dim(value, 0, width, axis=dim)
        before = lax.ppermute(last, axis, up)
        after = lax.ppermute(first, axis, down)
        value = jnp.concatenate([before, value, after], axis=dim)
    return value


def from_behind(block, axis, distance):
    devices = range(lax.axis_size(axis))
    route = [(i - distance, i) for i in devices if i - distance in devices]
    return lax.ppermute(block, axis, route)


def split_tables(length):
    indices = np.arange(length)
    angles = (indices[:, None] * indices[None, :] % length) * (2.0 * np.pi / length)
    cos_table = np.cos(angles) / np.sqrt(length)
    sin_table = np.sin(angles) / np.sqrt(length)
    forward = np.block([[cos_table, sin_table], [-sin_table, cos_table]])
    inverse = np.block([[cos_table, -sin_table], [sin_table, cos_table]])

    def halves(table):
        coarse = table.astype(np.float32).astype(ml_dtypes.bfloat16)
        fine = (table - coarse.astype(np.float64)).astype(ml_dtypes.bfloat16)
        return (coarse, fine)

    lefts, rights = ([], [])
    for left, right in ((forward, inverse), (inverse, forward)):
        coarse, fine = halves(left)
        lefts.append(np.concatenate([coarse, fine, coarse], axis=1))
        coarse, fine = halves(right)
        rights.append(np.concatenate([coarse, coarse, fine], axis=0))
    return (np.stack(lefts), np.stack(rights))


def halve(value):
    coarse = value.astype(jnp.bfloat16)
    return (coarse, (value - coarse.astype(jnp.float32)).astype(jnp.bfloat16))


def multiply(left, right):
    return jnp.dot(left, right, preferred_element_type=jnp.float32)


def from_left(table, value):
    coarse, fine = halve(value)
    return multiply(table, jnp.concatenate([coarse, coarse, fine], axis=0))


def from_right(value, table):
    coarse, fine = halve(value)
    return multiply(jnp.concatenate([coarse, fine, coarse], axis=1), table)


def regroup(value, length):
    top, bottom = (value[:length], value[length:])
    return jnp.concatenate(
        [
            jnp.concatenate([top[:, :length], bottom[:, :length]], axis=1),
            jnp.concatenate([top[:, length:], bottom[:, length:]], axis=1),
        ],
        axis=0,
    )


def slots_kernel(
    starts, counts, object_map, probes, intensity, lefts, rights, totals, sums, window, far, lit
):
    modes, length = (probes.shape[1], probes.shape[-1])
    breadth = object_map.shape[-1]
    tall = length // 8
    sublane = lax.broadcasted_iota(jnp.int32, (tall, 8, length), 1)
    sublane_more = lax.broadcasted_iota(jnp.int32, (tall + 1, 8, length), 1)
    totals[...] = jnp.zeros_like(totals)
    sums[...] = jnp.zeros_like(sums)
    lighting = jnp.zeros((length, length), jnp.float32)
    for mode in range(modes):
        lighting += probes[0, mode] * probes[0, mode] + probes[1, mode] * probes[1, mode]
    lit[...] = lighting

    def visit_slot(slot, carry):
        row, col = (starts[slot, 0], starts[slot, 1])
        tile = jnp.minimum(row // 8, object_map.shape[1] - tall - 1)
        shift = row - 8 * tile
        back = lax.rem(breadth - col, breadth)
        for plane in range(2):
            wide = object_map[plane, pl.ds(tile, tall + 1)]
            wide = pltpu.roll(wide, back, 2)[:, :, :length]
            wide = pltpu.roll(wide, lax.rem(8 - shift, 8), 1)
            wide = jnp.where(sublane + shift < 8, wide[:tall], wide[1:])
            window[plane] = wide.reshape(length, length)
        modelled = jnp.zeros((length, length), jnp.float32)
        for pair in range(modes // 2):
            obj_r, obj_i = (window[0], window[1])
            waves_r, waves_i = ([], [])
            for mode in (2 * pair, 2 * pair + 1):
                waves_r.append(probes[0, mode] * obj_r - probes[1, mode] * obj_i)
                waves_i.append(probes[0, mode] * obj_i + probes[1, mode] * obj_r)
            wave = jnp.concatenate(
                [jnp.concatenate(waves_r, axis=1), jnp.concatenate(waves_i, axis=1)], axis=0
            )
            half = regroup(from_left(lefts[0], wave), length)
            spread = from_right(half, rights[0])
            far[pair] = spread
            power = spread * spread
            power = power[:, :length] + power[:, length:]
            modelled += power[:length] + power[length:]
        factor = jnp.sqrt(intensity[slot] / jnp.maximum(modelled, 1.0)) - 1.0
        factor = jnp.concatenate([factor, factor], axis=1)
        factor = jnp.concatenate([factor, factor], axis=0)
        terms_r = jnp.zeros((length, length), jnp.float32)
        terms_i = jnp.zeros((length, length), jnp.float32)
        for pair in range(modes // 2):
            half = regroup(from_right(far[pair] * factor, rights[1]), length)
            change = from_left(lefts[1], half)
            obj_r, obj_i = (window[0], window[1])
            for which in range(2):
                mode = 2 * pair + which
                lanes = slice(which * length, (which + 1) * length)
                change_r, change_i = (change[:length, lanes], change[length:, lanes])
                probe_r, probe_i = (probes[0, mode], probes[1, mode])
                terms_r += probe_r * change_r + probe_i * change_i
                terms_i += probe_r * change_i - probe_i * change_r
                sums[mode] += obj_r * change_r + obj_i * change_i
                sums[modes + mode] += obj_r * change_i - obj_i * change_r
        sums[2 * modes] += window[0] * window[0] + window[1] * window[1]
        blank = jnp.zeros((1, 8, length), jnp.float32)
        margin = jnp.zeros((tall + 1, 8, breadth - length), jnp.float32)
        for plane, terms in enumerate((terms_r, terms_i, lit[...])):
            terms = pltpu.roll(terms.reshape(tall, 8, length), lax.rem(shift, 8), 1)
            terms = jnp.where(
                sublane_more >= shift,
                jnp.concatenate([terms, blank], axis=0),
                jnp.concatenate([blank, terms], axis=0),
            )
            wide = pltpu.roll(jnp.concatenate([terms, margin], axis=2), col, 2)
            totals[plane, pl.ds(tile, tall + 1)] += wide
        return carry

    lax.fori_loop(0, counts[0], visit_slot, 0)


def accumulate(object_map, probes, starts, counts, intensity, lefts, rights):
    _, modes, length, _ = probes.shape
    _, height, breadth = object_map.shape
    memory = pl.BlockSpec(memory_space=pltpu.VMEM)
    scalars = pl.BlockSpec(memory_space=pltpu.SMEM)
    totals, sums = pl.pallas_call(
        slots_kernel,
        out_shape=(
            jax.ShapeDtypeStruct((3, height // 8, 8, breadth), jnp.float32),
            jax.ShapeDtypeStruct((2 * modes + 1, length, length), jnp.float32),
        ),
        in_specs=[scalars, scalars] + [memory] * 5,
        out_specs=(memory, memory),
        scratch_shapes=[
            pltpu.VMEM((2, length, length), jnp.float32),
            pltpu.VMEM((modes // 2, 2 * length, 2 * length), jnp.float32),
            pltpu.VMEM((length, length), jnp.float32),
        ],
        compiler_params=pltpu.CompilerParams(vmem_limit_bytes=40 * 1024 * 1024),
        name="slots",
    )(starts, counts, object_map.reshape(2, height // 8, 8, breadth), probes, intensity, lefts, rights)
    return (totals.reshape(3, height, breadth), sums)


def mixing(probes, probe_step):
    mix_r = jnp.sum(probes[0] * probe_step[0] + probes[1] * probe_step[1], axis=0)
    mix_i = jnp.sum(probes[0] * probe_step[1] - probes[1] * probe_step[0], axis=0)
    return (mix_r, mix_i)


def cross_term(object_map, change, starts, active, mix_r, mix_i):
    length = mix_r.shape[-1]
    anchor_index = jnp.int32(0)

    def cross_visit_slot(running, element):
        corner_at, weight = element
        corner = (anchor_index, corner_at[0], corner_at[1])
        object_win = lax.dynamic_slice(object_map, corner, (2, length, length))
        change_win = lax.dynamic_slice(change, corner, (2, length, length))
        aligned = change_win[0] * object_win[0] + change_win[1] * object_win[1]
        rotated = change_win[0] * object_win[1] - change_win[1] * object_win[0]
        return (running + weight * jnp.sum(aligned * mix_r - rotated * mix_i), None)

    running, _ = lax.scan(cross_visit_slot, jnp.zeros((), jnp.float32), (starts, active))
    return running


def solve_steps(object_curve, cross_curve, probe_curve, object_slope, probe_slope):
    object_diag = 1.1 * object_curve + 0.001
    probe_diag = 1.1 * probe_curve + 0.001
    determinant = object_diag * probe_diag - cross_curve * cross_curve
    object_rate = (probe_diag * object_slope - cross_curve * probe_slope) / determinant
    probe_rate = (object_diag * probe_slope - cross_curve * object_slope) / determinant
    return (object_rate, probe_rate)


def widen(planes, margin):
    return with_halo(planes, (("tx", 1), ("ty", 2)), margin)


def fold_rims(totals, margin, height, breadth):
    middle = totals[:, margin : margin + height, :]
    for direction in (1, -1):
        border = totals[:, margin + height :, :] if direction == 1 else totals[:, :margin, :]
        arrived = from_behind(border, "tx", direction)
        if direction == 1:
            middle = jnp.concatenate([middle + arrived, middle[:, margin:, :]], axis=1)
        else:
            middle = jnp.concatenate([middle[:, : height - margin, :], middle + arrived], axis=1)
    interior = middle[:, :, margin : margin + breadth]
    for direction in (1, -1):
        border = middle[:, :, margin + breadth :] if direction == 1 else middle[:, :, :margin]
        arrived = from_behind(border, "ty", direction)
        if direction == 1:
            interior = jnp.concatenate(
                [interior[:, :, :margin] + arrived, interior[:, :, margin:]], axis=2
            )
        else:
            interior = jnp.concatenate(
                [interior[:, :, : breadth - margin], interior[:, :, breadth - margin :] + arrived],
                axis=2,
            )
    return interior


def shards(object_field, probe_modes, positions, counts, intensity):
    length = probe_modes.shape[-1]
    margin = length // 2
    height = object_field.shape[1]
    breadth = object_field.shape[2]
    lefts, rights = split_tables(length)
    modes = probe_modes.shape[1]
    anchor = jnp.stack(
        [lax.axis_index("tx") * height - margin, lax.axis_index("ty") * breadth - margin]
    )
    starts = positions - anchor[None, :]
    active = (jnp.arange(positions.shape[0], dtype=jnp.int32) < counts[0]).astype(jnp.float32)
    object_map = object_field
    probes = probe_modes
    extended = widen(object_map, margin)
    for repeat in range(ITERS):
        totals, sums = accumulate(extended, probes, starts, counts, intensity, lefts, rights)
        interior = fold_rims(totals, margin, height, breadth)
        change = interior[:2] / jnp.maximum(interior[2], 1.0)
        object_part = jnp.sum((change[0] * change[0] + change[1] * change[1]) * interior[2])
        slope_part = jnp.sum(interior[:2] * change)
        wide_change = widen(change, margin)
        sums = lax.psum(sums, ("tx", "ty"))
        probe_total = sums[: 2 * modes].reshape(probes.shape)
        weight_total = sums[2 * modes]
        probe_step = probe_total / (weight_total + 1e-05)
        mix_r, mix_i = mixing(probes, probe_step)
        cross_part = cross_term(extended, wide_change, starts, active, mix_r, mix_i)
        object_curve, cross_curve, object_slope = lax.psum(
            (object_part, cross_part, slope_part), ("tx", "ty")
        )
        probe_curve = jnp.sum(
            (probe_step[0] * probe_step[0] + probe_step[1] * probe_step[1]) * weight_total
        )
        probe_slope = jnp.sum(probe_total * probe_step)
        object_rate, probe_rate = solve_steps(
            object_curve, cross_curve, probe_curve, object_slope, probe_slope
        )
        object_map = object_map + object_rate * change
        probes = probes + probe_rate * probe_step
        if repeat + 1 < ITERS:
            extended = extended + object_rate * wide_change
    return (object_map, probes)


def solution(mesh):
    return jax.shard_map(
        shards,
        mesh=mesh,
        in_specs=(
            P("groups", "tx", "ty"),
            P("groups", None, None, None),
            P(("groups", "tx", "ty"), None),
            P(("groups", "tx", "ty")),
            P(("groups", "tx", "ty"), None, None),
        ),
        out_specs=(P("groups", "tx", "ty"), P("groups", None, None, None)),
        check_vma=False,
    )
```

profile of v0, /device:TPU:0, one launch (start us, length us, event | category | flops | bytes accessed | tf_op | source)
XLA Modules:
  0.0 465.8 jit_solution(14066532555124595434)
XLA Ops:
  7.2 1.4 collective-permute-start.1
  8.7 5.6 %collective-permute-start = (f32[2,64,128]{2,1,0:T(8,128)}, f32[2,64,128]{2,1,0:T(8,128)S(1)}, u32[]{:S(2)}, u32[]{:S(2)}) collective-permute-start(f32[2,64,128]{2,1,0:T(8,128)} %param.11), channel_id=1, source_target_pairs={{0,4},{4,8},{8,12},{1,5},{5,9},{9,13},{2,6},{6,10},{10,14},{3,7},{... | collective-permute-start | bytes 196616 | tf_op jit(solution)/shard_map/ppermute | solution.py:20
  15.1 1.4 collective-permute-done
  17.4 1.3 collective-permute-start.2
  18.7 1.3 collective-permute-start.3
  20.7 3.5 collective-permute-done.3
  24.5 1.1 copy-done.2
  25.6 1.0 copy-done.4
  26.6 19.6 %slots.2 = (f32[3,24,8,256]{3,2,1,0:T(8,128)S(1)}, f32[17,128,128]{2,1,0:T(8,128)}) custom-call(s32[6,2]{1,0:T(8,128)S(1)} %broadcast_subtract_fusion.starts, s32[1]{0:T(128)} %copy.29.counts, f32[2,24,8,256]{3,2,1,0:T(8,128)S(1)} %fusion.26.object_map, f32[2,8,128,128]{3,2,1,0:T(8,128)S(1)} %copy-done, f32[6,128,128]{2,1,0:T(8,128)S(1)} %copy-done.4, ...), custom_call_target="tpu_custom_call" | custom-call | tf_op jit(solution)/shard_map/slots/pallas_call | solution.py:166
  46.2 1.3 collective-permute-start.4
  47.5 1.3 collective-permute-start.5
  48.8 1.9 collective-permute-done.4
  50.6 6.8 %collective-permute-done.5 = f32[3,64,256]{2,1,0:T(8,128)S(1)} collective-permute-done((f32[3,64,256]{2,1,0:T(8,128)S(1)}, f32[3,64,256]{2,1,0:T(8,128)S(1)}, u32[]{:S(2)}, u32[]{:S(2)}) %collective-permute-start.5) | collective-permute-done | bytes 196640 | tf_op jit(solution)/shard_map/ppermute | solution.py:29
  57.6 4.9 %collective-permute-start.6 = (f32[3,64,64]{2,1,0:T(8,128)S(1)}, f32[3,64,64]{2,1,0:T(8,128)S(1)}, u32[]{:S(2)}, u32[]{:S(2)}) collective-permute-start(f32[3,64,64]{2,1,0:T(8,128)S(1)} %slice.248), channel_id=1, source_target_pairs={{0,1},{1,2},{2,3},{4,5},{5,6},{6,7},{8,9},{9,10},{10,11},{12,13},{... | collective-permute-start | bytes 147464 | tf_op jit(solution)/shard_map/ppermute | solution.py:29
  62.5 0.9 collective-permute-done.6
  63.5 1.3 collective-permute-start.7
  65.0 1.9 collective-permute-done.7
  67.8 1.3 collective-permute-start.9
  69.1 4.5 collective-permute-start.8
  74.0 1.6 collective-permute-done.8
  76.4 4.9 %collective-permute-start.10 = (f32[2,192,64]{2,1,0:T(8,128)S(1)}, f32[2,192,64]{2,1,0:T(8,128)S(1)}, u32[]{:S(2)}, u32[]{:S(2)}) collective-permute-start(f32[2,192,64]{2,1,0:T(8,128)S(1)} %get-tuple-element.178), channel_id=1, source_target_pairs={{0,1},{1,2},{2,3},{4,5},{5,6},{6,7},{8,9},{9,10},{10,11},{12,13},{... | collective-permute-start | bytes 294920 | tf_op jit(solution)/shard_map/ppermute | solution.py:20
  81.3 1.3 collective-permute-start.11
  83.2 2.3 collective-permute-done.11
  86.4 74.6 %all-reduce.5.cloned.1.call-done = f32[17,128,128]{2,1,0:T(8,128)} async-done(((f32[17,128,128]{2,1,0:T(8,128)}), f32[17,128,128]{2,1,0:T(8,128)}) %all-reduce.5.cloned.1.call-update) | async-done | bytes 1114128 | tf_op jit(solution)/shard_map/psum | solution.py:268
  161.9 2.2 fusion.4
  164.1 1.0 copy-done.7
  166.9 42.4 %while.20 = (s32[]{:T(128)}, f32[]{:T(128)}, f32[6]{0:T(128)S(1)}, s32[6,2]{0,1:T(2,128)S(1)}, f32[2,192,256]{2,1,0:T(8,128)S(1)}, /*index=5*/f32[2,192,256]{2,1...) while((s32[]{:T(128)}, f32[]{:T(128)}, f32[6]{0:T(128)S(1)}, ...), condition=%wide.region_8.9_spmd, body=%wide.region_6.0_spmd.sunk | while | flops 163850 | bytes 393517 | solution.py:204
  209.9 32.5 %all-reduce.1 = (f32[]{:T(128)}, f32[]{:T(128)}, f32[]{:T(128)}) all-reduce(f32[]{:T(128)} %get-tuple-element.158, f32[]{:T(128)} %get-tuple-element.92, f32[]{:T(128)} %fusion.17), channel_id=1, replica_groups=mesh['groups'=2,'tx'=4,'ty'=4] {'tx','ty'}, use_global_device_ids=true, to_apply=%region_3.0 | all-reduce | flops 3 | bytes 24 | tf_op jit(solution)/shard_map/psum | solution.py:274
  247.9 1.4 multiply_add_fusion.1.probes
  250.6 18.9 %slots.3 = (f32[3,24,8,256]{3,2,1,0:T(8,128)S(1)}, f32[17,128,128]{2,1,0:T(8,128)S(1)}) custom-call(s32[6,2]{1,0:T(8,128)S(1)} %broadcast_subtract_fusion.starts, s32[1]{0:T(128)} %copy.29.counts, f32[2,24,8,256]{3,2,1,0:T(8,128)S(1)} %maximum_add_fusion.object_map, f32[2,8,128,128]{3,2,1,0:T(8,128)S(1)} %multiply_add_fusion.1.probes, ...), custom_call_target="tpu_custom_call" | custom-call | tf_op jit(solution)/shard_map/slots/pallas_call | solution.py:166
  269.5 1.3 collective-permute-start.12
  270.8 1.3 collective-permute-start.13
  272.1 1.9 collective-permute-done.12
  274.0 4.4 collective-permute-done.13
  278.6 1.4 collective-permute-start.14
  281.0 1.3 collective-permute-start.15
  282.3 1.9 collective-permute-done.15
  285.0 1.3 collective-permute-start.17
  286.3 4.5 collective-permute-start.16
  291.3 1.5 collective-permute-done.16
  292.9 4.4 collective-permute-start.18
  297.3 1.3 collective-permute-start.19
  299.3 1.5 collective-permute-done.19
  301.0 72.6 %all-reduce.7.cloned.1.call-done = f32[17,128,128]{2,1,0:T(8,128)} async-done(((f32[17,128,128]{2,1,0:T(8,128)}), f32[17,128,128]{2,1,0:T(8,128)}) %all-reduce.7.cloned.1.call-update) | async-done | bytes 1114128 | tf_op jit(solution)/shard_map/psum | solution.py:268
  374.5 2.1 fusion.5
  379.1 39.8 %while.21 = (s32[]{:T(128)}, f32[]{:T(128)}, f32[6]{0:T(128)S(1)}, s32[6,2]{0,1:T(2,128)S(1)}, f32[2,192,256]{2,1,0:T(8,128)S(1)}, /*index=5*/f32[2,192,256]{2,1...) while((s32[]{:T(128)}, f32[]{:T(128)}, f32[6]{0:T(128)S(1)}, ...), condition=%wide.region_21.22_spmd, body=%wide.region_19.0_spmd.sunk | while | flops 163850 | bytes 393517 | solution.py:204
  419.0 32.4 %all-reduce = (f32[]{:T(128)}, f32[]{:T(128)}, f32[]{:T(128)}) all-reduce(f32[]{:T(128)} %get-tuple-element.154, f32[]{:T(128)} %get-tuple-element.95, f32[]{:T(128)} %fusion.14), channel_id=1, replica_groups=mesh['groups'=2,'tx'=4,'ty'=4] {'tx','ty'}, use_global_device_ids=true, to_apply=%region_16.17 | all-reduce | flops 3 | bytes 24 | tf_op jit(solution)/shard_map/psum | solution.py:274
  457.2 1.1 multiply_add_fusion
  (148 shorter events, 40.5 us)
Async XLA Ops:
  7.2 17.3 %copy-start.1 = (bf16[2,768,256]{2,1,0:T(8,128)(2,1)S(1)}, bf16[2,768,256]{2,1,0:T(8,128)(2,1)}, u32[]{:S(2)}) copy-start(bf16[2,768,256]{2,1,0:T(8,128)(2,1)} %constant.58.clone.rights) | copy-start | bytes 2359300
  7.2 17.3 %copy-start = (f32[2,8,128,128]{3,2,1,0:T(8,128)S(1)}, f32[2,8,128,128]{3,2,1,0:T(8,128)}, u32[]{:S(2)}) copy-start(f32[2,8,128,128]{3,2,1,0:T(8,128)} %probes.1) | copy-start | bytes 3145732
  7.2 153.8 %all-reduce.5.cloned.1.call-start = ((), (), s32[]{:S(2)}) async-start(), calls=%async_computation | async-start | bytes 2228224 | tf_op jit(solution)/shard_map/psum | solution.py:268
  7.2 10.1 %collective-permute-start.1 = (f32[2,64,128]{2,1,0:T(8,128)}, f32[2,64,128]{2,1,0:T(8,128)S(1)}, u32[]{:S(2)}, u32[]{:S(2)}) collective-permute-start(f32[2,64,128]{2,1,0:T(8,128)} %param.11), channel_id=1, source_target_pairs={{4,0},{8,4},{12,8},{5,1},{9,5},{13,9},{6,2},{10,6},{14,10},{7,3},{... | collective-permute-start | bytes 196616 | tf_op jit(solution)/shard_map/ppermute | solution.py:21
  8.7 7.8 %collective-permute-start = (f32[2,64,128]{2,1,0:T(8,128)}, f32[2,64,128]{2,1,0:T(8,128)S(1)}, u32[]{:S(2)}, u32[]{:S(2)}) collective-permute-start(f32[2,64,128]{2,1,0:T(8,128)} %param.11), channel_id=1, source_target_pairs={{0,4},{4,8},{8,12},{1,5},{5,9},{9,13},{2,6},{6,10},{10,14},{3,7},{... | collective-permute-start | bytes 196616 | tf_op jit(solution)/shard_map/ppermute | solution.py:20
  17.4 3.3 collective-permute-start.2
  18.7 5.5 %collective-permute-start.3 = (f32[2,192,64]{2,1,0:T(8,128)S(1)}, f32[2,192,64]{2,1,0:T(8,128)S(1)}, u32[]{:S(2)}, u32[]{:S(2)}) collective-permute-start(f32[2,192,64]{2,1,0:T(8,128)S(1)} %get-tuple-element.185), channel_id=1, source_target_pairs={{1,0},{2,1},{3,2},{5,4},{6,5},{7,6},{9,8},{10,9},{11,10},{13,12},{... | collective-permute-start | bytes 294920 | tf_op jit(solution)/shard_map/ppermute | solution.py:21
  24.5 1.1 copy-start.2
  25.6 1.0 copy-start.4
  46.2 4.5 collective-permute-start.4
  47.5 10.0 %collective-permute-start.5 = (f32[3,64,256]{2,1,0:T(8,128)S(1)}, f32[3,64,256]{2,1,0:T(8,128)S(1)}, u32[]{:S(2)}, u32[]{:S(2)}) collective-permute-start(f32[3,64,256]{2,1,0:T(8,128)S(1)} %get-tuple-element.173), channel_id=1, source_target_pairs={{4,0},{8,4},{12,8},{5,1},{9,5},{13,9},{6,2},{10,6},{14,10},{7,3},{... | collective-permute-start | bytes 589832 | tf_op jit(solution)/shard_map/ppermute | solution.py:29
  57.6 5.8 %collective-permute-start.6 = (f32[3,64,64]{2,1,0:T(8,128)S(1)}, f32[3,64,64]{2,1,0:T(8,128)S(1)}, u32[]{:S(2)}, u32[]{:S(2)}) collective-permute-start(f32[3,64,64]{2,1,0:T(8,128)S(1)} %slice.248), channel_id=1, source_target_pairs={{0,1},{1,2},{2,3},{4,5},{5,6},{6,7},{8,9},{9,10},{10,11},{12,13},{... | collective-permute-start | bytes 147464 | tf_op jit(solution)/shard_map/ppermute | solution.py:29
  63.5 3.4 collective-permute-start.7
  65.0 308.6 %all-reduce.7.cloned.1.call-start = ((), (), s32[]{:S(2)}) async-start(), calls=%async_computation.1 | async-start | bytes 2228224 | tf_op jit(solution)/shard_map/psum | solution.py:268
  67.8 6.1 %collective-permute-start.9 = (f32[2,64,128]{2,1,0:T(8,128)S(1)}, f32[2,64,128]{2,1,0:T(8,128)S(1)}, u32[]{:S(2)}, u32[]{:S(2)}) collective-permute-start(f32[2,64,128]{2,1,0:T(8,128)S(1)} %get-tuple-element.159), channel_id=1, source_target_pairs={{4,0},{8,4},{12,8},{5,1},{9,5},{13,9},{6,2},{10,6},{14,10},{7,3},{... | collective-permute-start | bytes 196616 | tf_op jit(solution)/shard_map/ppermute | solution.py:21
  69.1 6.4 %collective-permute-start.8 = (f32[2,64,128]{2,1,0:T(8,128)S(1)}, f32[2,64,128]{2,1,0:T(8,128)S(1)}, u32[]{:S(2)}, u32[]{:S(2)}) collective-permute-start(f32[2,64,128]{2,1,0:T(8,128)S(1)} %get-tuple-element.159), channel_id=1, source_target_pairs={{0,4},{4,8},{8,12},{1,5},{5,9},{9,13},{2,6},{6,10},{10,14},{3,7},{... | collective-permute-start | bytes 196616 | tf_op jit(solution)/shard_map/ppermute | solution.py:20
  74.0 11.6 %copy-start.18 = (f32[2,64,128]{2,1,0:T(8,128)}, f32[2,64,128]{2,1,0:T(8,128)S(1)}, u32[]{:S(2)}) copy-start(f32[2,64,128]{2,1,0:T(8,128)S(1)} %collective-permute-done.9) | copy-start | bytes 196612
  75.5 10.0 %copy-start.20 = (f32[2,64,128]{2,1,0:T(8,128)}, f32[2,64,128]{2,1,0:T(8,128)S(1)}, u32[]{:S(2)}) copy-start(f32[2,64,128]{2,1,0:T(8,128)S(1)} %collective-permute-done.8) | copy-start | bytes 196612
  76.4 6.8 %collective-permute-start.10 = (f32[2,192,64]{2,1,0:T(8,128)S(1)}, f32[2,192,64]{2,1,0:T(8,128)S(1)}, u32[]{:S(2)}, u32[]{:S(2)}) collective-permute-start(f32[2,192,64]{2,1,0:T(8,128)S(1)} %get-tuple-element.178), channel_id=1, source_target_pairs={{0,1},{1,2},{2,3},{4,5},{5,6},{6,7},{8,9},{9,10},{10,11},{12,13},{... | collective-permute-start | bytes 294920 | tf_op jit(solution)/shard_map/ppermute | solution.py:20
  81.3 4.2 collective-permute-start.11
  83.2 80.9 %copy-start.8 = (f32[2,192,64]{2,1,0:T(8,128)}, f32[2,192,64]{2,1,0:T(8,128)S(1)}, u32[]{:S(2)}) copy-start(f32[2,192,64]{2,1,0:T(8,128)S(1)} %collective-permute-done.10) | copy-start | bytes 294916
  85.5 0.7 copy-start.11
  161.9 2.2 copy-start.16
  164.1 1.0 copy-start.7
  247.9 1.5 copy-start.9
  247.9 1.5 copy-start.12
  247.9 1.5 copy-start.17
  249.4 1.1 copy-start.3
  249.4 1.2 copy-start.5
  269.5 11.5 %copy-start.6 = (f32[17,128,128]{2,1,0:T(8,128)}, f32[17,128,128]{2,1,0:T(8,128)S(1)}, u32[]{:S(2)}) copy-start(f32[17,128,128]{2,1,0:T(8,128)S(1)} %get-tuple-element.93) | copy-start | bytes 3342340
  269.5 4.5 collective-permute-start.12
  270.8 7.6 %collective-permute-start.13 = (f32[3,64,256]{2,1,0:T(8,128)S(1)}, f32[3,64,256]{2,1,0:T(8,128)S(1)}, u32[]{:S(2)}, u32[]{:S(2)}) collective-permute-start(f32[3,64,256]{2,1,0:T(8,128)S(1)} %get-tuple-element.171), channel_id=1, source_target_pairs={{4,0},{8,4},{12,8},{5,1},{9,5},{13,9},{6,2},{10,6},{14,10},{7,3},{... | collective-permute-start | bytes 589832 | tf_op jit(solution)/shard_map/ppermute | solution.py:29
  278.5 12.4 %copy-start.10 = (f32[2,192,64]{2,1,0:T(8,128)S(1)}, f32[2,192,64]{2,1,0:T(8,128)}, u32[]{:S(2)}) copy-start(f32[2,192,64]{2,1,0:T(8,128)} %copy-done.8) | copy-start | bytes 294916
  278.5 12.4 %copy-start.13 = (f32[2,192,64]{2,1,0:T(8,128)S(1)}, f32[2,192,64]{2,1,0:T(8,128)}, u32[]{:S(2)}) copy-start(f32[2,192,64]{2,1,0:T(8,128)} %copy-done.11) | copy-start | bytes 294916
  278.5 12.4 %copy-start.19 = (f32[2,64,128]{2,1,0:T(8,128)S(1)}, f32[2,64,128]{2,1,0:T(8,128)}, u32[]{:S(2)}) copy-start(f32[2,64,128]{2,1,0:T(8,128)} %copy-done.18) | copy-start | bytes 196612
  278.6 12.4 %copy-start.21 = (f32[2,64,128]{2,1,0:T(8,128)S(1)}, f32[2,64,128]{2,1,0:T(8,128)}, u32[]{:S(2)}) copy-start(f32[2,64,128]{2,1,0:T(8,128)} %copy-done.20) | copy-start | bytes 196612
  278.6 2.4 collective-permute-start.14
  281.0 3.2 collective-permute-start.15
  285.0 15.7 %copy-start.14 = (f32[2,64,128]{2,1,0:T(8,128)}, f32[2,64,128]{2,1,0:T(8,128)S(1)}, u32[]{:S(2)}) copy-start(f32[2,64,128]{2,1,0:T(8,128)S(1)} %get-tuple-element.155) | copy-start | bytes 196612
  285.0 6.3 %collective-permute-start.17 = (f32[2,64,128]{2,1,0:T(8,128)S(1)}, f32[2,64,128]{2,1,0:T(8,128)S(1)}, u32[]{:S(2)}, u32[]{:S(2)}) collective-permute-start(f32[2,64,128]{2,1,0:T(8,128)S(1)} %get-tuple-element.155), channel_id=1, source_target_pairs={{4,0},{8,4},{12,8},{5,1},{9,5},{13,9},{6,2},{10,6},{14,10},{7,3},{... | collective-permute-start | bytes 196616 | tf_op jit(solution)/shard_map/ppermute | solution.py:21
  286.3 6.5 %collective-permute-start.16 = (f32[2,64,128]{2,1,0:T(8,128)S(1)}, f32[2,64,128]{2,1,0:T(8,128)S(1)}, u32[]{:S(2)}, u32[]{:S(2)}) collective-permute-start(f32[2,64,128]{2,1,0:T(8,128)S(1)} %get-tuple-element.155), channel_id=1, source_target_pairs={{0,4},{4,8},{8,12},{1,5},{5,9},{9,13},{2,6},{6,10},{10,14},{3,7},{... | collective-permute-start | bytes 196616 | tf_op jit(solution)/shard_map/ppermute | solution.py:20
  292.9 6.4 %collective-permute-start.18 = (f32[2,192,64]{2,1,0:T(8,128)S(1)}, f32[2,192,64]{2,1,0:T(8,128)S(1)}, u32[]{:S(2)}, u32[]{:S(2)}) collective-permute-start(f32[2,192,64]{2,1,0:T(8,128)S(1)} %get-tuple-element.174), channel_id=1, source_target_pairs={{0,1},{1,2},{2,3},{4,5},{5,6},{6,7},{8,9},{9,10},{10,11},{12,13},{... | collective-permute-start | bytes 294920 | tf_op jit(solution)/shard_map/ppermute | solution.py:20
  297.3 3.4 collective-permute-start.19
  457.2 1.2 copy-start.15
  457.2 1.2 copy-start.22
Sparse Core Ops, SparseCore 0:
  65.1 95.8 all-reduce.4
  282.5 91.1 all-reduce.6
where the time goes:
time: 469 us; the launch traced here: 466 us
  waiting for transfers between devices  180 us (38%)
  blocking collectives  64.9 us (14%)
  loops' own time  58.4 us (12%)
  starting transfers between devices  47.3 us (10%)
  Pallas kernels  38.4 us (8%)
  between operations  27.8 us (6%)
  other arithmetic  25.9 us (6%)
  local copies, waits for them, and re-layouts  23.4 us (5%)
    psum x2, waiting for transfers between devices, shards(): sums = lax.psum(sums, ('tx', 'ty'))  147 us
    psum x2, blocking collectives, shards(): lax.psum((object_part, cross_part, slope_part), ('tx', 'ty'))  64.9 us
    another operation x2, loops' own time, cross_term(): lax.scan(cross_visit_slot, jnp.zeros((), jnp.float32), (starts, active))  58.4 us
    pallas_call x2, Pallas kernels, accumulate(): pl.pallas_call(slots_kernel, out_shape=(jax.ShapeDtypeStruct((3, height /...  38.4 us
    ppermute x6, starting transfers between devices, with_halo(): before = lax.ppermute(last, axis, up)  25.3 us
    ppermute x8, waiting for transfers between devices, from_behind(): return lax.ppermute(block, axis, route)  20.6 us
    ppermute x8, starting transfers between devices, from_behind(): return lax.ppermute(block, axis, route)  14.1 us
  transfers between devices with their start and end apart: 22, of which 17 were waited for; matrix products, arithmetic and copies ran while one was open for 1% of the time, Pallas kernels for 0%

commit v1 on v0

--- a/solution.py
+++ b/solution.py
@@ -1,3 +1,5 @@
+import functools
+
 import jax
 import jax.numpy as jnp
 import ml_dtypes
@@ -8,6 +10,8 @@
 from jax.sharding import PartitionSpec as P
 
 ITERS = 2
+memory = pl.BlockSpec(memory_space=pltpu.VMEM)
+scalars = pl.BlockSpec(memory_space=pltpu.SMEM)
 
 
 def with_halo(value, sides, width):
@@ -82,11 +86,12 @@
 
 
 def slots_kernel(
-    starts, counts, object_map, probes, intensity, lefts, rights, totals, sums, window, far, lit
+    lead, starts, counts, object_map, probes, intensity, lefts, rights, totals, sums, window, far, lit
 ):
     modes, length = (probes.shape[1], probes.shape[-1])
     breadth = object_map.shape[-1]
     tall = length // 8
+    per = modes // 2
     sublane = lax.broadcasted_iota(jnp.int32, (tall, 8, length), 1)
     sublane_more = lax.broadcasted_iota(jnp.int32, (tall + 1, 8, length), 1)
     totals[...] = jnp.zeros_like(totals)
@@ -100,7 +105,8 @@
         row, col = (starts[slot, 0], starts[slot, 1])
         tile = jnp.minimum(row // 8, object_map.shape[1] - tall - 1)
         shift = row - 8 * tile
-        back = lax.rem(breadth - col, breadth)
+        back = lax.rem(breadth + lead - col, breadth)
+        onward = lax.rem(breadth - lead + col, breadth)
         for plane in range(2):
             wide = object_map[plane, pl.ds(tile, tall + 1)]
             wide = pltpu.roll(wide, back, 2)[:, :, :length]
@@ -139,9 +145,12 @@
                 probe_r, probe_i = (probes[0, mode], probes[1, mode])
                 terms_r += probe_r * change_r + probe_i * change_i
                 terms_i += probe_r * change_i - probe_i * change_r
-                sums[mode] += obj_r * change_r + obj_i * change_i
-                sums[modes + mode] += obj_r * change_i - obj_i * change_r
-        sums[2 * modes] += window[0] * window[0] + window[1] * window[1]
+                stream, place = (mode // per, mode % per)
+                sums[stream, place] += obj_r * change_r + obj_i * change_i
+                sums[stream, per + place] += obj_r * change_i - obj_i * change_r
+        coverage = window[0] * window[0] + window[1] * window[1]
+        sums[0, 2 * per] += coverage
+        sums[1, 2 * per] += coverage
         blank = jnp.zeros((1, 8, length), jnp.float32)
         margin = jnp.zeros((tall + 1, 8, breadth - length), jnp.float32)
         for plane, terms in enumerate((terms_r, terms_i, lit[...])):
@@ -151,23 +160,20 @@
                 jnp.concatenate([terms, blank], axis=0),
                 jnp.concatenate([blank, terms], axis=0),
             )
-            wide = pltpu.roll(jnp.concatenate([terms, margin], axis=2), col, 2)
+            wide = pltpu.roll(jnp.concatenate([terms, margin], axis=2), onward, 2)
             totals[plane, pl.ds(tile, tall + 1)] += wide
         return carry
 
     lax.fori_loop(0, counts[0], visit_slot, 0)
 
 
-def accumulate(object_map, probes, starts, counts, intensity, lefts, rights):
+def accumulate(object_map, probes, starts, counts, intensity, lefts, rights, lead):
     _, modes, length, _ = probes.shape
-    _, height, breadth = object_map.shape
-    memory = pl.BlockSpec(memory_space=pltpu.VMEM)
-    scalars = pl.BlockSpec(memory_space=pltpu.SMEM)
-    totals, sums = pl.pallas_call(
-        slots_kernel,
+    return pl.pallas_call(
+        functools.partial(slots_kernel, lead),
         out_shape=(
-            jax.ShapeDtypeStruct((3, height // 8, 8, breadth), jnp.float32),
-            jax.ShapeDtypeStruct((2 * modes + 1, length, length), jnp.float32),
+            jax.ShapeDtypeStruct((3,) + object_map.shape[1:], jnp.float32),
+            jax.ShapeDtypeStruct((2, modes + 1, length, length), jnp.float32),
         ),
         in_specs=[scalars, scalars] + [memory] * 5,
         out_specs=(memory, memory),
@@ -178,8 +184,7 @@
         ],
         compiler_params=pltpu.CompilerParams(vmem_limit_bytes=40 * 1024 * 1024),
         name="slots",
-    )(starts, counts, object_map.reshape(2, height // 8, 8, breadth), probes, intensity, lefts, rights)
-    return (totals.reshape(3, height, breadth), sums)
+    )(starts, counts, object_map, probes, intensity, lefts, rights)
 
 
 def mixing(probes, probe_step):
@@ -243,7 +248,7 @@
     return interior
 
 
-def shards(object_field, probe_modes, positions, counts, intensity):
+def general(object_field, probe_modes, positions, counts, intensity):
     length = probe_modes.shape[-1]
     margin = length // 2
     height = object_field.shape[1]
@@ -259,15 +264,18 @@
     probes = probe_modes
     extended = widen(object_map, margin)
     for repeat in range(ITERS):
-        totals, sums = accumulate(extended, probes, starts, counts, intensity, lefts, rights)
+        tiled = extended.reshape(2, -1, 8, extended.shape[-1])
+        totals, sums = accumulate(tiled, probes, starts, counts, intensity, lefts, rights, 0)
+        totals = totals.reshape((3,) + extended.shape[1:])
         interior = fold_rims(totals, margin, height, breadth)
         change = interior[:2] / jnp.maximum(interior[2], 1.0)
         object_part = jnp.sum((change[0] * change[0] + change[1] * change[1]) * interior[2])
         slope_part = jnp.sum(interior[:2] * change)
         wide_change = widen(change, margin)
         sums = lax.psum(sums, ("tx", "ty"))
-        probe_total = sums[: 2 * modes].reshape(probes.shape)
-        weight_total = sums[2 * modes]
+        probe_total = sums[:, :modes].reshape(2, 2, modes // 2, length, length)
+        probe_total = jnp.swapaxes(probe_total, 0, 1).reshape(probes.shape)
+        weight_total = sums[0, modes]
         probe_step = probe_total / (weight_total + 1e-05)
         mix_r, mix_i = mixing(probes, probe_step)
         cross_part = cross_term(extended, wide_change, starts, active, mix_r, mix_i)
@@ -288,6 +296,385 @@
     return (object_map, probes)
 
 
+def greet(peers):
+    barrier = pltpu.get_barrier_semaphore()
+    for peer in peers:
+        pl.semaphore_signal(barrier, 1, device_id=peer, device_id_type=pl.DeviceIdType.MESH)
+    pl.semaphore_wait(barrier, len(peers))
+
+
+def everyone(row, col):
+    return [
+        {"tx": (row + i) % 4, "ty": (col + j) % 4} for i in range(4) for j in range(4) if i or j
+    ]
+
+
+AROUND = [(i, j) for i in (-1, 0, 1) for j in (-1, 0, 1) if i or j]
+
+
+def around(row, col, what):
+    for k, (i, j) in enumerate(AROUND):
+        inside = (row + i >= 0) & (row + i < 4) & (col + j >= 0) & (col + j < 4)
+        pl.when(inside)(functools.partial(what, k, i, j))
+
+
+def copy_to(source, target, send, arrive, index, peer):
+    return pltpu.make_async_remote_copy(
+        src_ref=source,
+        dst_ref=target,
+        send_sem=send.at[index],
+        recv_sem=arrive.at[index],
+        device_id=peer,
+        device_id_type=pl.DeviceIdType.MESH,
+    )
+
+
+def halo_copy(block, halo, send, arrive, base, row, col, k, i, j):
+    opposite = AROUND.index((-i, -j))
+    return pltpu.make_async_remote_copy(
+        src_ref=block,
+        dst_ref=halo.at[opposite],
+        send_sem=send.at[base + k],
+        recv_sem=arrive.at[base + opposite],
+        device_id={"tx": row + i, "ty": col + j},
+        device_id_type=pl.DeviceIdType.MESH,
+    )
+
+
+def halo_wait(block, halo, send, arrive, base, row, col, k, i, j):
+    halo_copy(block, halo, send, arrive, base, row, col, k, i, j).wait_send()
+    pltpu.make_async_remote_copy(
+        src_ref=block,
+        dst_ref=halo.at[k],
+        send_sem=send.at[base + k],
+        recv_sem=arrive.at[base + k],
+        device_id={"tx": row + i, "ty": col + j},
+        device_id_type=pl.DeviceIdType.MESH,
+    ).wait_recv()
+
+
+def spread_halo(own, halo, wide):
+    high, broad = (own.shape[1], own.shape[-1])
+    early = lax.broadcasted_iota(jnp.int32, own.shape, 3) < broad // 2
+    for i in (-1, 0, 1):
+        rows = slice((i + 1) * high, (i + 2) * high)
+        middle = own if i == 0 else halo[AROUND.index((i, 0))]
+        wide[:, rows, :, :broad] = middle
+        wide[:, rows, :, broad:] = jnp.where(
+            early, halo[AROUND.index((i, 1))], halo[AROUND.index((i, -1))]
+        )
+
+
+def widen_kernel(own, wide, halo, send, arrive):
+    row, col = (lax.axis_index("tx"), lax.axis_index("ty"))
+    halo[...] = jnp.zeros_like(halo)
+    greet(everyone(row, col))
+    common = (own, halo, send, arrive, 0, row, col)
+    around(row, col, lambda k, i, j: halo_copy(*common, k, i, j).start())
+    around(row, col, lambda k, i, j: halo_wait(*common, k, i, j))
+    spread_halo(own[...], halo, wide)
+
+
+def widen_tiles(own):
+    two, high, _, broad = own.shape
+    return pl.pallas_call(
+        widen_kernel,
+        out_shape=jax.ShapeDtypeStruct((two, 3 * high, 8, 2 * broad), jnp.float32),
+        in_specs=[memory],
+        out_specs=memory,
+        scratch_shapes=[
+            pltpu.VMEM((8,) + own.shape, jnp.float32),
+            pltpu.SemaphoreType.DMA((8,)),
+            pltpu.SemaphoreType.DMA((8,)),
+        ],
+        compiler_params=pltpu.CompilerParams(
+            collective_id=0, has_side_effects=True, vmem_limit_bytes=40 * 1024 * 1024
+        ),
+        name="widen",
+    )(own)
+
+
+def in_rows(values, lanes):
+    at = lax.broadcasted_iota(jnp.int32, (8, lanes), 0)
+    result = jnp.zeros((8, lanes), jnp.float32)
+    for place, value in enumerate(values):
+        result = jnp.where(at == place, value, result)
+    return result
+
+
+def combine_kernel(
+    totals, sums, wide, step, parts, rims, own, halo, r1, acc, ra2, acca, rb2, accb, ra3, rb3, got,
+    send, arrive,
+):
+    row, col = (lax.axis_index("tx"), lax.axis_index("ty"))
+    core, side = (col % 2, col // 2)
+    planes = step.shape[1]
+    high, broad = (own.shape[1], own.shape[-1])
+    rims[...] = jnp.zeros_like(rims)
+    halo[...] = jnp.zeros_like(halo)
+    greet(everyone(row, col))
+    partner = {"tx": row, "ty": side * 2 + (1 - core)}
+    across = {"tx": row, "ty": (1 - side) * 2 + core}
+    along = [{"tx": (row + j) % 4, "ty": col} for j in (1, 2, 3)]
+
+    first = copy_to(sums.at[:, :, pl.ds(8 * (1 - core), 8)], r1, send, arrive, 0, partner)
+    first.start()
+
+    def rim_source(i, j):
+        rows = slice((i + 1) * high, (i + 2) * high)
+        lanes = slice(0, broad) if j == 0 else slice(broad, 2 * broad)
+        return totals.at[:, rows, :, lanes]
+
+    fold = (rims, send, arrive, 24, row, col)
+    around(row, col, lambda k, i, j: halo_copy(rim_source(i, j), *fold, k, i, j).start())
+
+    first.wait()
+    acc[...] = sums[:, :, pl.ds(8 * core, 8)] + r1[...]
+    second = [copy_to(acc.at[0, :, pl.ds(4 * (1 - side), 4)], ra2, send, arrive, 1, across)]
+    for j in (1, 2, 3):
+        source = acc.at[1, :, pl.ds(2 * ((row + j) % 4), 2)]
+        second.append(copy_to(source, rb2.at[j - 1], send, arrive, 1 + j, along[j - 1]))
+    for copy in second:
+        copy.start()
+
+    around(row, col, lambda k, i, j: halo_wait(rim_source(i, j), *fold, k, i, j))
+    early = lax.broadcasted_iota(jnp.int32, (3,) + own.shape[1:], 3) < broad // 2
+    interior = totals[:, high : 2 * high, :, :broad]
+    for i in (-1, 1):
+        interior += rims[AROUND.index((i, 0))]
+    for i in (-1, 0, 1):
+        interior += jnp.where(early, rims[AROUND.index((i, -1))], rims[AROUND.index((i, 1))])
+    change = interior[:2] / jnp.maximum(interior[2], 1.0)
+    own[...] = change
+    spread = (own, halo, send, arrive, 32, row, col)
+    around(row, col, lambda k, i, j: halo_copy(*spread, k, i, j).start())
+    curve = jnp.sum((change[0] * change[0] + change[1] * change[1]) * interior[2])
+    slope = jnp.sum(interior[:2] * change)
+
+    for copy in second:
+        copy.wait()
+    acca[...] = acc[0, :, pl.ds(4 * side, 4)] + ra2[...]
+    accb[...] = acc[1, :, pl.ds(2 * row, 2)] + rb2[0] + rb2[1] + rb2[2]
+    third = [copy_to(accb.at[:, pl.ds(1 - side, 1)], rb3, send, arrive, 5, across)]
+    for j in (1, 2, 3):
+        source = acca.at[:, pl.ds((row + j) % 4, 1)]
+        third.append(copy_to(source, ra3.at[j - 1], send, arrive, 5 + j, along[j - 1]))
+    for copy in third:
+        copy.start()
+    for copy in third:
+        copy.wait()
+    sum_a = acca[:, pl.ds(row, 1)] + ra3[0] + ra3[1] + ra3[2]
+    sum_b = accb[:, pl.ds(side, 1)] + rb3[...]
+    at_a = 8 * core + 4 * side + row
+    at_b = 8 * core + 2 * row + side
+    probe_curve, probe_slope = (jnp.float32(0.0), jnp.float32(0.0))
+    for stream, (total, at) in enumerate(((sum_a, at_a), (sum_b, at_b))):
+        weight = total[planes:]
+        found = total[:planes] / (weight + 1e-05)
+        got[stream, :, pl.ds(at, 1)] = found
+        probe_curve += jnp.sum(found * found * weight)
+        probe_slope += jnp.sum(total[:planes] * found)
+
+    def give(stream, at, count, index, peer):
+        block = got.at[stream, :, pl.ds(at, count)]
+        return copy_to(block, block, send, arrive, index, peer)
+
+    fourth = [give(1, at_b, 1, 9, across)]
+    for j in (1, 2, 3):
+        fourth.append(give(0, at_a, 1, 9 + j, along[j - 1]))
+    for copy in fourth:
+        copy.start()
+    for copy in fourth:
+        copy.wait()
+    fifth = [give(0, 8 * core + 4 * side, 4, 13, across)]
+    for j in (1, 2, 3):
+        fifth.append(give(1, 8 * core + 2 * row, 2, 13 + j, along[j - 1]))
+    for copy in fifth:
+        copy.start()
+    parts[...] = in_rows((curve, slope, probe_curve, probe_slope), parts.shape[-1])
+    around(row, col, lambda k, i, j: halo_wait(*spread, k, i, j))
+    spread_halo(own[...], halo, wide)
+    for copy in fifth:
+        copy.wait()
+    block = got.at[:, :, pl.ds(8 * core, 8)]
+    last = copy_to(block, block, send, arrive, 17, partner)
+    last.start()
+    last.wait()
+    step[...] = got[...]
+
+
+def combine(totals, sums):
+    _, rows, _, lanes = totals.shape
+    planes = sums.shape[1] - 1
+    length = sums.shape[-1]
+    high, broad = (rows // 3, lanes // 2)
+    f32 = jnp.float32
+    both = planes + 1
+    return pl.pallas_call(
+        combine_kernel,
+        out_shape=(
+            jax.ShapeDtypeStruct((2, rows, 8, lanes), f32),
+            jax.ShapeDtypeStruct((2, planes, 16, 8, length), f32),
+            jax.ShapeDtypeStruct((8, length), f32),
+        ),
+        in_specs=[memory] * 2,
+        out_specs=(memory,) * 3,
+        scratch_shapes=[
+            pltpu.VMEM((8, 3, high, 8, broad), f32),
+            pltpu.VMEM((2, high, 8, broad), f32),
+            pltpu.VMEM((8, 2, high, 8, broad), f32),
+            pltpu.VMEM((2, both, 8, 8, length), f32),
+            pltpu.VMEM((2, both, 8, 8, length), f32),
+            pltpu.VMEM((both, 4, 8, length), f32),
+            pltpu.VMEM((both, 4, 8, length), f32),
+            pltpu.VMEM((3, both, 2, 8, length), f32),
+            pltpu.VMEM((both, 2, 8, length), f32),
+            pltpu.VMEM((3, both, 1, 8, length), f32),
+            pltpu.VMEM((both, 1, 8, length), f32),
+            pltpu.VMEM((2, planes, 16, 8, length), f32),
+            pltpu.SemaphoreType.DMA((40,)),
+            pltpu.SemaphoreType.DMA((40,)),
+        ],
+        compiler_params=pltpu.CompilerParams(
+            collective_id=1, has_side_effects=True, vmem_limit_bytes=40 * 1024 * 1024
+        ),
+        name="combine",
+    )(totals, sums.reshape(2, both, 16, 8, length))
+
+
+def cross_kernel(starts, counts, object_map, change, probes, step, parts, result, product, held):
+    length, modes, lanes = (probes.shape[-1], probes.shape[1], object_map.shape[-1])
+    per, tall = (modes // 2, length // 8)
+    lead = lanes // 4
+    product[0] = change[0] * object_map[0] + change[1] * object_map[1]
+    product[1] = change[0] * object_map[1] - change[1] * object_map[0]
+    held[...] = jnp.zeros_like(held)
+    sublane = lax.broadcasted_iota(jnp.int32, (tall, 8, length), 1)
+
+    def visit_slot(slot, carry):
+        row, col = (starts[slot, 0], starts[slot, 1])
+        tile = jnp.minimum(row // 8, object_map.shape[1] - tall - 1)
+        shift = row - 8 * tile
+        back = lax.rem(lanes + lead - col, lanes)
+        for plane in range(2):
+            wide = product[plane, pl.ds(tile, tall + 1)]
+            wide = pltpu.roll(wide, back, 2)[:, :, :length]
+            wide = pltpu.roll(wide, lax.rem(8 - shift, 8), 1)
+            held[plane] += jnp.where(sublane + shift < 8, wide[:tall], wide[1:])
+        return carry
+
+    lax.fori_loop(0, counts[0], visit_slot, 0)
+    mix_r = jnp.zeros(held.shape[1:], jnp.float32)
+    mix_i = jnp.zeros(held.shape[1:], jnp.float32)
+    for mode in range(modes):
+        stream, place = (mode // per, mode % per)
+        step_r, step_i = (step[stream, place], step[stream, per + place])
+        mix_r += probes[0, mode] * step_r + probes[1, mode] * step_i
+        mix_i += probes[0, mode] * step_i - probes[1, mode] * step_r
+    cross = jnp.sum(held[0] * mix_r - held[1] * mix_i)
+    at = lax.broadcasted_iota(jnp.int32, parts.shape, 0)
+    result[...] = jnp.where(at == 4, cross, parts[...])
+
+
+def cross(starts, counts, object_map, change, probes, step, parts):
+    return pl.pallas_call(
+        cross_kernel,
+        out_shape=jax.ShapeDtypeStruct(parts.shape, jnp.float32),
+        in_specs=[scalars, scalars] + [memory] * 5,
+        out_specs=memory,
+        scratch_shapes=[
+            pltpu.VMEM(object_map.shape, jnp.float32),
+            pltpu.VMEM((2,) + probes.shape[2:], jnp.float32),
+        ],
+        compiler_params=pltpu.CompilerParams(vmem_limit_bytes=40 * 1024 * 1024),
+        name="cross",
+    )(starts, counts, object_map, change, probes, step, parts)
+
+
+def advance_kernel(parts, object_map, change, probes, step, new_map, new_probes, inbox, send, arrive):
+    row, col = (lax.axis_index("tx"), lax.axis_index("ty"))
+    peers = everyone(row, col)
+    greet(peers)
+    copies = [
+        copy_to(parts, inbox.at[k], send, arrive, k, peer) for k, peer in enumerate(peers)
+    ]
+    for copy in copies:
+        copy.start()
+    for copy in copies:
+        copy.wait()
+    modes = probes.shape[1]
+    per = modes // 2
+    total = parts[...] + jnp.sum(inbox[...], axis=0)
+    object_curve, object_slope = (total[0:1], total[1:2])
+    probe_curve, probe_slope = (total[2:3], total[3:4])
+    object_rate, probe_rate = solve_steps(
+        object_curve, total[4:5], probe_curve, object_slope, probe_slope
+    )
+    object_rate = jnp.broadcast_to(object_rate, (8, parts.shape[-1]))
+    probe_rate = jnp.broadcast_to(probe_rate, (8, parts.shape[-1]))
+    rates = jnp.concatenate([object_rate, object_rate], axis=1)
+    new_map[...] = object_map[...] + rates * change[...]
+    for mode in range(modes):
+        stream, place = (mode // per, mode % per)
+        new_probes[0, mode] = probes[0, mode] + probe_rate * step[stream, place]
+        new_probes[1, mode] = probes[1, mode] + probe_rate * step[stream, per + place]
+
+
+def advance(parts, object_map, change, probes, step):
+    return pl.pallas_call(
+        advance_kernel,
+        out_shape=(
+            jax.ShapeDtypeStruct(object_map.shape, jnp.float32),
+            jax.ShapeDtypeStruct(probes.shape, jnp.float32),
+        ),
+        in_specs=[memory] * 5,
+        out_specs=(memory, memory),
+        scratch_shapes=[
+            pltpu.VMEM((15,) + parts.shape, jnp.float32),
+            pltpu.SemaphoreType.DMA((15,)),
+            pltpu.SemaphoreType.DMA((15,)),
+        ],
+        compiler_params=pltpu.CompilerParams(
+            collective_id=2, has_side_effects=True, vmem_limit_bytes=40 * 1024 * 1024
+        ),
+        name="advance",
+    )(parts, object_map, change, probes, step)
+
+
+def direct(object_field, probe_modes, positions, counts, intensity):
+    two, modes, length, _ = probe_modes.shape
+    margin = length // 2
+    _, height, breadth = object_field.shape
+    lefts, rights = split_tables(length)
+    anchor = jnp.stack(
+        [lax.axis_index("tx") * height - margin, lax.axis_index("ty") * breadth - margin]
+    )
+    starts = positions - anchor[None, :]
+    object_map = widen_tiles(object_field.reshape(2, height // 8, 8, breadth))
+    probes = probe_modes
+    for _ in range(ITERS):
+        totals, sums = accumulate(
+            object_map, probes, starts, counts, intensity, lefts, rights, margin
+        )
+        change, step, parts = combine(totals, sums)
+        tiles = probes.reshape(2, modes, length // 8, 8, length)
+        parts = cross(starts, counts, object_map, change, tiles, step, parts)
+        object_map, tiles = advance(parts, object_map, change, tiles, step)
+        probes = tiles.reshape(probes.shape)
+    own = object_map[:, height // 8 : height // 4, :, :breadth]
+    return (own.reshape(object_field.shape), probes)
+
+
+def shards(object_field, probe_modes, positions, counts, intensity):
+    _, height, breadth = object_field.shape
+    length = probe_modes.shape[-1]
+    grid = (lax.axis_size("tx"), lax.axis_size("ty"))
+    arguments = (object_field, probe_modes, positions, counts, intensity)
+    if grid == (4, 4) and length == 128 and (2 * height, breadth) == (length, length):
+        return direct(*arguments)
+    return general(*arguments)
+
+
 def solution(mesh):
     return jax.shard_map(
         shards,

time: 469 us -> 148 us (0.32)
  waiting for transfers between devices: 180 us -> 0 us
  Pallas kernels: 38.4 us -> 137 us
  blocking collectives: 64.9 us -> 0 us
  loops' own time: 58.4 us -> 0 us
  starting transfers between devices: 47.3 us -> 0 us
  between operations: 27.8 us -> 1.43 us
  other arithmetic: 25.9 us -> 0.08 us
  local copies, waits for them, and re-layouts: 23.4 us -> 7.71 us
    psum x2 -> x0, waiting for transfers between devices: 147 us -> none  [shards(): sums = lax.psum(sums, ('tx', 'ty'))]
    pallas_call x2 -> x9, Pallas kernels: 38.4 us -> 137 us  [the longest x2 102 us: combine(): pl.pallas_call(combine_kernel, out_shape=(jax.ShapeDtypeStruct((2, rows,...]
    psum x2 -> x0, blocking collectives: 64.9 us -> none  [shards(): lax.psum((object_part, cross_part, slope_part), ('tx', 'ty'))]
    another operation x2 -> x0, loops' own time: 58.4 us -> none  [cross_term(): lax.scan(cross_visit_slot, jnp.zeros((), jnp.float32), (starts, active))]
    ppermute x20 -> x0, starting transfers between devices: 47.2 us -> none  [the longest x6 25.3 us: with_halo(): before = lax.ppermute(last, axis, up)]
    ppermute x20 -> x0, waiting for transfers between devices: 32.4 us -> none  [the longest x8 20.6 us: from_behind(): return lax.ppermute(block, axis, route)]
    reduce_sum x22 -> x0, other arithmetic: 18 us -> none  [the longest x12 9.05 us: cross_visit_slot(): return (running + weight * jnp.sum(aligned * mix_r - rotated * mix_i), None)]
    dynamic_slice x24 -> x0, local copies, waits for them, and re-layouts: 8.14 us -> none  [cross_term(): lax.scan(cross_visit_slot, jnp.zeros((), jnp.float32), (starts, active))]
  transfers between devices with their start and end apart: 22 -> 0, of which waited for: 17 -> 0; matrix products, arithmetic and copies ran while one was open for 1% -> 0% of each run, Pallas kernels for 0% -> 0%
where the time goes in v1:
time: 148 us; the launch traced here: 147 us
  Pallas kernels  137 us (93%)
  local copies, waits for them, and re-layouts  7.71 us (5%)
    pallas_call x2, Pallas kernels, combine(): pl.pallas_call(combine_kernel, out_shape=(jax.ShapeDtypeStruct((2, rows,...  102 us
    pallas_call x2, Pallas kernels, advance(): pl.pallas_call(advance_kernel, out_shape=(jax.ShapeDtypeStruct(object_map...  15.5 us
    pallas_call x1, Pallas kernels, widen_tiles(): pl.pallas_call(widen_kernel, out_shape=jax.ShapeDtypeStruct((two, 3 * hig...  10.1 us
    pallas_call x2, Pallas kernels, accumulate(): pl.pallas_call(functools.partial(slots_kernel, lead), out_shape=(jax.Shap...  7.85 us
    unnamed x20, local copies, waits for them, and re-layouts  7.08 us

profile of v1, /device:TPU:0, one launch (start us, length us, event | category | flops | bytes accessed | tf_op | source)
XLA Modules:
  0.0 146.7 jit_solution(14141528436060232527)
XLA Ops:
  1.3 0.1 pad_add_fusion
  1.4 0.8 copy.9
  2.1 0.0 copy-start.8
  2.1 0.8 copy-done.8
  3.0 10.1 %widen.1.object_map = f32[2,24,8,256]{3,2,1,0:T(8,128)S(1)} custom-call(f32[2,8,8,128]{3,2,1,0:T(8,128)S(1)} %bitcast.16), custom_call_target="tpu_custom_call" | custom-call | tf_op jit(solution)/shard_map/widen/pallas_call | solution.py:380
  13.0 0.0 copy-start
  13.1 1.2 copy-done
  14.3 0.0 copy-start.2
  14.3 1.1 copy-done.2
  15.4 0.0 copy-start.4
  15.4 1.1 copy-done.4
  16.5 0.0 copy-start.6
  16.5 1.0 copy-done.6
  17.5 3.9 %slots.2 = (f32[3,24,8,256]{3,2,1,0:T(8,128)S(1)}, f32[2,9,128,128]{3,2,1,0:T(8,128)S(1)}) custom-call(s32[6,2]{1,0:T(8,128)S(1)} %broadcast_subtract_fusion.starts, s32[1]{0:T(128)S(6)} %copy.11.counts, f32[2,24,8,256]{3,2,1,0:T(8,128)S(1)} %widen.1.object_map, f32[2,8,128,128]{3,2,1,0:T(8,128)S(1)} %copy-done, f32[6,128,128]{2,1,0:T(8,128)S(1)} %copy-done.6, ...), custom_call_target="tpu_custom_call" | custom-call | tf_op jit(solution)/shard_map/slots/pallas_call | solution.py:172
  21.5 0.0 copy-start.1
  21.5 51.3 %combine.2 = (f32[2,24,8,256]{3,2,1,0:T(8,128)S(1)}, f32[2,8,16,8,128]{4,3,2,1,0:T(8,128)S(1)}, f32[8,128]{1,0:T(8,128)S(1)}) custom-call(f32[3,24,8,256]{3,2,1,0:T(8,128)S(1)} %get-tuple-element.16.totals, f32[2,9,16,8,128]{4,3,2,1,0:T(8,128)S(1)} %bitcast.14), custom_call_target="tpu_custom_call" | custom-call | tf_op jit(solution)/shard_map/combine/pallas_call | solution.py:513
  72.8 0.0 copy-done.1
  72.8 1.2 cross.2.parts
  74.0 0.0 copy-start.3
  74.0 0.0 copy-start.5
  74.0 0.0 copy-start.7
  74.0 7.7 %advance.2 = (f32[2,24,8,256]{3,2,1,0:T(8,128)S(1)}, f32[2,8,16,8,128]{4,3,2,1,0:T(8,128)S(1)}) custom-call(f32[8,128]{1,0:T(8,128)S(1)} %cross.2.parts, f32[2,24,8,256]{3,2,1,0:T(8,128)S(1)} %widen.1.object_map, f32[2,24,8,256]{3,2,1,0:T(8,128)S(1)} %get-tuple-element.18.change, f32[2,8,16,8,128]{4,3,2,1,0:T(8,128)S(1)} %bitcast.11, ...), custom_call_target="tpu_custom_call" | custom-call | tf_op jit(solution)/shard_map/advance/pallas_call | solution.py:624
  81.8 0.0 copy-done.3
  81.8 0.0 copy-done.5
  81.8 0.0 copy-done.7
  81.8 3.9 %slots.3 = (f32[3,24,8,256]{3,2,1,0:T(8,128)S(1)}, f32[2,9,128,128]{3,2,1,0:T(8,128)S(1)}) custom-call(s32[6,2]{1,0:T(8,128)S(1)} %broadcast_subtract_fusion.starts, s32[1]{0:T(128)S(6)} %copy.11.counts, f32[2,24,8,256]{3,2,1,0:T(8,128)S(1)} %get-tuple-element.21.object_map, f32[2,8,128,128]{3,2,1,0:T(8,128)S(1)} %bitcast.12, f32[6,128,128]{2,1,0:T(8,128)S(1)} %copy-done.7, ...), custom_call_target="tpu_custom_call" | custom-call | tf_op jit(solution)/shard_map/slots/pallas_call | solution.py:172
  85.7 50.4 %combine.3 = (f32[2,24,8,256]{3,2,1,0:T(8,128)S(1)}, f32[2,8,16,8,128]{4,3,2,1,0:T(8,128)S(1)}, f32[8,128]{1,0:T(8,128)S(1)}) custom-call(f32[3,24,8,256]{3,2,1,0:T(8,128)S(1)} %get-tuple-element.23.totals, f32[2,9,16,8,128]{4,3,2,1,0:T(8,128)S(1)} %bitcast.13), custom_call_target="tpu_custom_call" | custom-call | tf_op jit(solution)/shard_map/combine/pallas_call | solution.py:513
  136.1 1.2 cross.3.parts
  137.4 7.7 %advance.3 = (f32[2,24,8,256]{3,2,1,0:T(8,128)S(1)}, f32[2,8,16,8,128]{4,3,2,1,0:T(8,128)S(1)}) custom-call(f32[8,128]{1,0:T(8,128)S(1)} %cross.3.parts, f32[2,24,8,256]{3,2,1,0:T(8,128)S(1)} %get-tuple-element.21.object_map, f32[2,24,8,256]{3,2,1,0:T(8,128)S(1)} %get-tuple-element.25.change, f32[2,8,16,8,128]{4,3,2,1,0:T(8,128)S(1)} %get-tuple-element.22.probes, ...), custom_call_target="tpu_custom_call" | custom-call | tf_op jit(solution)/shard_map/advance/pallas_call | solution.py:624
  145.1 0.6 slice_bitcast_fusion
  145.7 1.0 copy.12
  (1 shorter events, 0.0 us)
Async XLA Ops:
  2.1 0.8 copy-start.8
  13.0 1.2 copy-start
  14.3 1.1 copy-start.2
  15.4 1.1 copy-start.4
  16.5 1.0 copy-start.6
  21.5 51.3 %copy-start.1 = (f32[2,8,128,128]{3,2,1,0:T(8,128)S(1)}, f32[2,8,128,128]{3,2,1,0:T(8,128)}, u32[]{:S(2)}) copy-start(f32[2,8,128,128]{3,2,1,0:T(8,128)} %probes.1) | copy-start | bytes 3145732
  74.0 7.8 %copy-start.3 = (bf16[2,768,256]{2,1,0:T(8,128)(2,1)S(1)}, bf16[2,768,256]{2,1,0:T(8,128)(2,1)}, u32[]{:S(2)}) copy-start(bf16[2,768,256]{2,1,0:T(8,128)(2,1)} %constant.19.clone.rights) | copy-start | bytes 2359300
  74.0 7.8 %copy-start.5 = (bf16[2,256,768]{2,1,0:T(8,128)(2,1)S(1)}, bf16[2,256,768]{2,1,0:T(8,128)(2,1)}, u32[]{:S(2)}) copy-start(bf16[2,256,768]{2,1,0:T(8,128)(2,1)} %constant.18.clone.lefts) | copy-start | bytes 2359300
  74.0 7.8 %copy-start.7 = (f32[6,128,128]{2,1,0:T(8,128)S(1)}, f32[6,128,128]{2,1,0:T(8,128)}, u32[]{:S(2)}) copy-start(f32[6,128,128]{2,1,0:T(8,128)} %intensity.3) | copy-start | bytes 1179652

commit v2 on v1

--- a/solution.py
+++ b/solution.py
@@ -402,16 +402,50 @@
     return result
 
 
+class Edges:
+    def __init__(self, axis, source, target, base):
+        self.axis, self.source, self.target, self.base = (axis, source, target, base)
+
+    def each(self, what):
+        here = lax.axis_index(self.axis)
+        for k, ahead in ((0, -1), (1, 1)):
+            peer = {"tx": lax.axis_index("tx"), "ty": lax.axis_index("ty")}
+            peer[self.axis] = here + ahead
+            pl.when((here + ahead >= 0) & (here + ahead < 4))(functools.partial(what, k, peer))
+
+    def copy(self, k, landing, peer, send, arrive):
+        return pltpu.make_async_remote_copy(
+            src_ref=self.source(k),
+            dst_ref=self.target(landing),
+            send_sem=send.at[self.base + k],
+            recv_sem=arrive.at[self.base + landing],
+            device_id=peer,
+            device_id_type=pl.DeviceIdType.MESH,
+        )
+
+    def start(self, send, arrive):
+        self.each(lambda k, peer: self.copy(k, 1 - k, peer, send, arrive).start())
+
+    def wait(self, send, arrive):
+        def finish(k, peer):
+            self.copy(k, 1 - k, peer, send, arrive).wait_send()
+            self.copy(k, k, peer, send, arrive).wait_recv()
+
+        self.each(finish)
+
+
 def combine_kernel(
-    totals, sums, wide, step, parts, rims, own, halo, r1, acc, ra2, acca, rb2, accb, ra3, rb3, got,
+    totals, sums, wide, step, parts, beside, tall, over, column, near, r1, acc, ra2, acca, rb2, accb, ra3, rb3, got,
     send, arrive,
 ):
     row, col = (lax.axis_index("tx"), lax.axis_index("ty"))
     core, side = (col % 2, col // 2)
     planes = step.shape[1]
-    high, broad = (own.shape[1], own.shape[-1])
-    rims[...] = jnp.zeros_like(rims)
-    halo[...] = jnp.zeros_like(halo)
+    high, broad = (over.shape[2], over.shape[-1])
+    ends = (slice(0, high), slice(2 * high, 3 * high))
+    middle = slice(high, 2 * high)
+    for buffer in (beside, over, column, near):
+        buffer[...] = jnp.zeros_like(buffer)
     greet(everyone(row, col))
     partner = {"tx": row, "ty": side * 2 + (1 - core)}
     across = {"tx": row, "ty": (1 - side) * 2 + core}
@@ -420,13 +454,12 @@
     first = copy_to(sums.at[:, :, pl.ds(8 * (1 - core), 8)], r1, send, arrive, 0, partner)
     first.start()
 
-    def rim_source(i, j):
-        rows = slice((i + 1) * high, (i + 2) * high)
-        lanes = slice(0, broad) if j == 0 else slice(broad, 2 * broad)
-        return totals.at[:, rows, :, lanes]
-
-    fold = (rims, send, arrive, 24, row, col)
-    around(row, col, lambda k, i, j: halo_copy(rim_source(i, j), *fold, k, i, j).start())
+    broad_lanes = slice(broad, 2 * broad)
+    fold_side = Edges("ty", lambda k: totals.at[:, :, :, broad_lanes], lambda k: beside.at[k], 24)
+    fold_over = Edges("tx", lambda k: tall.at[:, ends[k]], lambda k: over.at[k], 26)
+    halo_over = Edges("tx", lambda k: column.at[:, middle], lambda k: column.at[:, ends[k]], 28)
+    halo_side = Edges("ty", lambda k: column, lambda k: near.at[k], 30)
+    fold_side.start(send, arrive)
 
     first.wait()
     acc[...] = sums[:, :, pl.ds(8 * core, 8)] + r1[...]
@@ -437,19 +470,10 @@
     for copy in second:
         copy.start()
 
-    around(row, col, lambda k, i, j: halo_wait(rim_source(i, j), *fold, k, i, j))
-    early = lax.broadcasted_iota(jnp.int32, (3,) + own.shape[1:], 3) < broad // 2
-    interior = totals[:, high : 2 * high, :, :broad]
-    for i in (-1, 1):
-        interior += rims[AROUND.index((i, 0))]
-    for i in (-1, 0, 1):
-        interior += jnp.where(early, rims[AROUND.index((i, -1))], rims[AROUND.index((i, 1))])
-    change = interior[:2] / jnp.maximum(interior[2], 1.0)
-    own[...] = change
-    spread = (own, halo, send, arrive, 32, row, col)
-    around(row, col, lambda k, i, j: halo_copy(*spread, k, i, j).start())
-    curve = jnp.sum((change[0] * change[0] + change[1] * change[1]) * interior[2])
-    slope = jnp.sum(interior[:2] * change)
+    fold_side.wait(send, arrive)
+    early = lax.broadcasted_iota(jnp.int32, tall.shape, 3) < broad // 2
+    tall[...] = totals[:, :, :, :broad] + jnp.where(early, beside[0], beside[1])
+    fold_over.start(send, arrive)
 
     for copy in second:
         copy.wait()
@@ -461,6 +485,13 @@
         third.append(copy_to(source, ra3.at[j - 1], send, arrive, 5 + j, along[j - 1]))
     for copy in third:
         copy.start()
+    fold_over.wait(send, arrive)
+    interior = tall[:, middle] + over[0] + over[1]
+    change = interior[:2] / jnp.maximum(interior[2], 1.0)
+    column[:, middle] = change
+    halo_over.start(send, arrive)
+    curve = jnp.sum((change[0] * change[0] + change[1] * change[1]) * interior[2])
+    slope = jnp.sum(interior[:2] * change)
     for copy in third:
         copy.wait()
     sum_a = acca[:, pl.ds(row, 1)] + ra3[0] + ra3[1] + ra3[2]
@@ -484,6 +515,8 @@
         fourth.append(give(0, at_a, 1, 9 + j, along[j - 1]))
     for copy in fourth:
         copy.start()
+    halo_over.wait(send, arrive)
+    halo_side.start(send, arrive)
     for copy in fourth:
         copy.wait()
     fifth = [give(0, 8 * core + 4 * side, 4, 13, across)]
@@ -492,8 +525,9 @@
     for copy in fifth:
         copy.start()
     parts[...] = in_rows((curve, slope, probe_curve, probe_slope), parts.shape[-1])
-    around(row, col, lambda k, i, j: halo_wait(*spread, k, i, j))
-    spread_halo(own[...], halo, wide)
+    halo_side.wait(send, arrive)
+    wide[:, :, :, :broad] = column[...]
+    wide[:, :, :, broad:] = jnp.where(early[:2], near[1], near[0])
     for copy in fifth:
         copy.wait()
     block = got.at[:, :, pl.ds(8 * core, 8)]
@@ -520,9 +554,11 @@
         in_specs=[memory] * 2,
         out_specs=(memory,) * 3,
         scratch_shapes=[
-            pltpu.VMEM((8, 3, high, 8, broad), f32),
-            pltpu.VMEM((2, high, 8, broad), f32),
-            pltpu.VMEM((8, 2, high, 8, broad), f32),
+            pltpu.VMEM((2, 3, rows, 8, broad), f32),
+            pltpu.VMEM((3, rows, 8, broad), f32),
+            pltpu.VMEM((2, 3, high, 8, broad), f32),
+            pltpu.VMEM((2, rows, 8, broad), f32),
+            pltpu.VMEM((2, 2, rows, 8, broad), f32),
             pltpu.VMEM((2, both, 8, 8, length), f32),
             pltpu.VMEM((2, both, 8, 8, length), f32),
             pltpu.VMEM((both, 4, 8, length), f32),

time: 148 us -> 139 us (0.939)
  Pallas kernels: 137 us -> 130 us
    pallas_call x2, Pallas kernels: 102 us -> 88 us  [combine(): pl.pallas_call(combine_kernel, out_shape=(jax.ShapeDtypeStruct((2, rows,...]
    pallas_call x2, Pallas kernels: 7.85 us -> 14.2 us  [accumulate(): pl.pallas_call(functools.partial(slots_kernel, lead), out_shape=(jax.Shap...]
where the time goes in v2:
time: 139 us
  Pallas kernels  130 us (94%)
  local copies, waits for them, and re-layouts  7.71 us (6%)
  between operations  1.43 us (1%)
    pallas_call x2, Pallas kernels, combine(): pl.pallas_call(combine_kernel, out_shape=(jax.ShapeDtypeStruct((2, rows,...  88 us
    pallas_call x2, Pallas kernels, advance(): pl.pallas_call(advance_kernel, out_shape=(jax.ShapeDtypeStruct(object_map...  14.9 us
    pallas_call x2, Pallas kernels, accumulate(): pl.pallas_call(functools.partial(slots_kernel, lead), out_shape=(jax.Shap...  14.2 us
    pallas_call x1, Pallas kernels, widen_tiles(): pl.pallas_call(widen_kernel, out_shape=jax.ShapeDtypeStruct((two, 3 * hig...  10.1 us
    unnamed x20, local copies, waits for them, and re-layouts  7.08 us

profile of v2, /device:TPU:0, one launch (start us, length us, event | category | flops | bytes accessed | tf_op | source)
XLA Modules:
  0.0 139.0 jit_solution(7788480728774148414)
XLA Ops:
  1.3 0.1 pad_add_fusion
  1.4 0.8 copy.9
  2.1 0.0 copy-start.8
  2.1 0.8 copy-done.8
  3.0 10.1 %widen.1.object_map = f32[2,24,8,256]{3,2,1,0:T(8,128)S(1)} custom-call(f32[2,8,8,128]{3,2,1,0:T(8,128)S(1)} %bitcast.16), custom_call_target="tpu_custom_call" | custom-call | tf_op jit(solution)/shard_map/widen/pallas_call | solution.py:380
  13.0 0.0 copy-start
  13.1 1.2 copy-done
  14.3 0.0 copy-start.2
  14.3 1.1 copy-done.2
  15.4 0.0 copy-start.4
  15.4 1.1 copy-done.4
  16.5 0.0 copy-start.6
  16.5 1.0 copy-done.6
  17.5 7.1 %slots.2 = (f32[3,24,8,256]{3,2,1,0:T(8,128)S(1)}, f32[2,9,128,128]{3,2,1,0:T(8,128)S(1)}) custom-call(s32[6,2]{1,0:T(8,128)S(1)} %broadcast_subtract_fusion.starts, s32[1]{0:T(128)S(6)} %copy.11.counts, f32[2,24,8,256]{3,2,1,0:T(8,128)S(1)} %widen.1.object_map, f32[2,8,128,128]{3,2,1,0:T(8,128)S(1)} %copy-done, f32[6,128,128]{2,1,0:T(8,128)S(1)} %copy-done.6, ...), custom_call_target="tpu_custom_call" | custom-call | tf_op jit(solution)/shard_map/slots/pallas_call | solution.py:172
  24.6 0.0 copy-start.1
  24.6 44.3 %combine.2 = (f32[2,24,8,256]{3,2,1,0:T(8,128)S(1)}, f32[2,8,16,8,128]{4,3,2,1,0:T(8,128)S(1)}, f32[8,128]{1,0:T(8,128)S(1)}) custom-call(f32[3,24,8,256]{3,2,1,0:T(8,128)S(1)} %get-tuple-element.16.totals, f32[2,9,16,8,128]{4,3,2,1,0:T(8,128)S(1)} %bitcast.14), custom_call_target="tpu_custom_call" | custom-call | tf_op jit(solution)/shard_map/combine/pallas_call | solution.py:547
  68.9 0.0 copy-done.1
  68.9 1.4 cross.2.parts
  70.3 0.0 copy-start.3
  70.3 0.0 copy-start.5
  70.3 0.0 copy-start.7
  70.3 7.5 %advance.2 = (f32[2,24,8,256]{3,2,1,0:T(8,128)S(1)}, f32[2,8,16,8,128]{4,3,2,1,0:T(8,128)S(1)}) custom-call(f32[8,128]{1,0:T(8,128)S(1)} %cross.2.parts, f32[2,24,8,256]{3,2,1,0:T(8,128)S(1)} %widen.1.object_map, f32[2,24,8,256]{3,2,1,0:T(8,128)S(1)} %get-tuple-element.18.change, f32[2,8,16,8,128]{4,3,2,1,0:T(8,128)S(1)} %bitcast.11, ...), custom_call_target="tpu_custom_call" | custom-call | tf_op jit(solution)/shard_map/advance/pallas_call | solution.py:660
  77.8 0.0 copy-done.3
  77.8 0.0 copy-done.5
  77.8 0.0 copy-done.7
  77.8 7.1 %slots.3 = (f32[3,24,8,256]{3,2,1,0:T(8,128)S(1)}, f32[2,9,128,128]{3,2,1,0:T(8,128)S(1)}) custom-call(s32[6,2]{1,0:T(8,128)S(1)} %broadcast_subtract_fusion.starts, s32[1]{0:T(128)S(6)} %copy.11.counts, f32[2,24,8,256]{3,2,1,0:T(8,128)S(1)} %get-tuple-element.21.object_map, f32[2,8,128,128]{3,2,1,0:T(8,128)S(1)} %bitcast.12, f32[6,128,128]{2,1,0:T(8,128)S(1)} %copy-done.7, ...), custom_call_target="tpu_custom_call" | custom-call | tf_op jit(solution)/shard_map/slots/pallas_call | solution.py:172
  84.9 43.7 %combine.3 = (f32[2,24,8,256]{3,2,1,0:T(8,128)S(1)}, f32[2,8,16,8,128]{4,3,2,1,0:T(8,128)S(1)}, f32[8,128]{1,0:T(8,128)S(1)}) custom-call(f32[3,24,8,256]{3,2,1,0:T(8,128)S(1)} %get-tuple-element.23.totals, f32[2,9,16,8,128]{4,3,2,1,0:T(8,128)S(1)} %bitcast.13), custom_call_target="tpu_custom_call" | custom-call | tf_op jit(solution)/shard_map/combine/pallas_call | solution.py:547
  128.7 1.4 cross.3.parts
  130.1 7.4 %advance.3 = (f32[2,24,8,256]{3,2,1,0:T(8,128)S(1)}, f32[2,8,16,8,128]{4,3,2,1,0:T(8,128)S(1)}) custom-call(f32[8,128]{1,0:T(8,128)S(1)} %cross.3.parts, f32[2,24,8,256]{3,2,1,0:T(8,128)S(1)} %get-tuple-element.21.object_map, f32[2,24,8,256]{3,2,1,0:T(8,128)S(1)} %get-tuple-element.25.change, f32[2,8,16,8,128]{4,3,2,1,0:T(8,128)S(1)} %get-tuple-element.22.probes, ...), custom_call_target="tpu_custom_call" | custom-call | tf_op jit(solution)/shard_map/advance/pallas_call | solution.py:660
  137.4 0.6 slice_bitcast_fusion
  138.1 1.0 copy.12
  (1 shorter events, 0.0 us)
Async XLA Ops:
  2.1 0.8 copy-start.8
  13.0 1.2 copy-start
  14.3 1.1 copy-start.2
  15.4 1.1 copy-start.4
  16.5 1.0 copy-start.6
  24.6 44.3 %copy-start.1 = (f32[2,8,128,128]{3,2,1,0:T(8,128)S(1)}, f32[2,8,128,128]{3,2,1,0:T(8,128)}, u32[]{:S(2)}) copy-start(f32[2,8,128,128]{3,2,1,0:T(8,128)} %probes.1) | copy-start | bytes 3145732
  70.3 7.5 %copy-start.3 = (bf16[2,768,256]{2,1,0:T(8,128)(2,1)S(1)}, bf16[2,768,256]{2,1,0:T(8,128)(2,1)}, u32[]{:S(2)}) copy-start(bf16[2,768,256]{2,1,0:T(8,128)(2,1)} %constant.19.clone.rights) | copy-start | bytes 2359300
  70.3 7.5 %copy-start.5 = (bf16[2,256,768]{2,1,0:T(8,128)(2,1)S(1)}, bf16[2,256,768]{2,1,0:T(8,128)(2,1)}, u32[]{:S(2)}) copy-start(bf16[2,256,768]{2,1,0:T(8,128)(2,1)} %constant.18.clone.lefts) | copy-start | bytes 2359300
  70.3 7.5 %copy-start.7 = (f32[6,128,128]{2,1,0:T(8,128)S(1)}, f32[6,128,128]{2,1,0:T(8,128)}, u32[]{:S(2)}) copy-start(f32[6,128,128]{2,1,0:T(8,128)} %intensity.3) | copy-start | bytes 1179652

commit v3 on v2

--- a/solution.py
+++ b/solution.py
@@ -388,8 +388,9 @@
             pltpu.SemaphoreType.DMA((8,)),
         ],
         compiler_params=pltpu.CompilerParams(
-            collective_id=0, has_side_effects=True, vmem_limit_bytes=40 * 1024 * 1024
+            collective_id=0, has_side_effects=True, vmem_limit_bytes=8 * 1024 * 1024
         ),
+        cost_estimate=pl.CostEstimate(flops=0, bytes_accessed=30_000_000, transcendentals=0),
         name="widen",
     )(own)
 
@@ -578,28 +579,33 @@
     )(totals, sums.reshape(2, both, 16, 8, length))
 
 
-def cross_kernel(starts, counts, object_map, change, probes, step, parts, result, product, held):
-    length, modes, lanes = (probes.shape[-1], probes.shape[1], object_map.shape[-1])
+def advance_kernel(
+    places, weights, object_map, change, probes, step, parts, new_map, new_probes, product, held, mine,
+    inbox, send, arrive,
+):
+    row, col = (lax.axis_index("tx"), lax.axis_index("ty"))
+    peers = everyone(row, col)
+    barrier = pltpu.get_barrier_semaphore()
+    for peer in peers:
+        pl.semaphore_signal(barrier, 1, device_id=peer, device_id_type=pl.DeviceIdType.MESH)
+    length, modes = (probes.shape[-1], probes.shape[1])
     per, tall = (modes // 2, length // 8)
-    lead = lanes // 4
     product[0] = change[0] * object_map[0] + change[1] * object_map[1]
     product[1] = change[0] * object_map[1] - change[1] * object_map[0]
     held[...] = jnp.zeros_like(held)
     sublane = lax.broadcasted_iota(jnp.int32, (tall, 8, length), 1)
 
     def visit_slot(slot, carry):
-        row, col = (starts[slot, 0], starts[slot, 1])
-        tile = jnp.minimum(row // 8, object_map.shape[1] - tall - 1)
-        shift = row - 8 * tile
-        back = lax.rem(lanes + lead - col, lanes)
+        tile, back = (places[slot, 0], places[slot, 1])
+        shift, upward, weight = (places[slot, 2], places[slot, 3], weights[slot])
         for plane in range(2):
-            wide = product[plane, pl.ds(tile, tall + 1)]
-            wide = pltpu.roll(wide, back, 2)[:, :, :length]
-            wide = pltpu.roll(wide, lax.rem(8 - shift, 8), 1)
-            held[plane] += jnp.where(sublane + shift < 8, wide[:tall], wide[1:])
+            part = product[plane, pl.ds(tile, tall + 1)]
+            part = pltpu.roll(part, back, 2)[:, :, :length]
+            part = pltpu.roll(part, upward, 1)
+            held[plane] += weight * jnp.where(sublane + shift < 8, part[:tall], part[1:])
         return carry
 
-    lax.fori_loop(0, counts[0], visit_slot, 0)
+    lax.fori_loop(0, places.shape[0], visit_slot, 0)
     mix_r = jnp.zeros(held.shape[1:], jnp.float32)
     mix_i = jnp.zeros(held.shape[1:], jnp.float32)
     for mode in range(modes):
@@ -609,42 +615,16 @@
         mix_i += probes[0, mode] * step_i - probes[1, mode] * step_r
     cross = jnp.sum(held[0] * mix_r - held[1] * mix_i)
     at = lax.broadcasted_iota(jnp.int32, parts.shape, 0)
-    result[...] = jnp.where(at == 4, cross, parts[...])
-
-
-def cross(starts, counts, object_map, change, probes, step, parts):
-    return pl.pallas_call(
-        cross_kernel,
-        out_shape=jax.ShapeDtypeStruct(parts.shape, jnp.float32),
-        in_specs=[scalars, scalars] + [memory] * 5,
-        out_specs=memory,
-        scratch_shapes=[
-            pltpu.VMEM(object_map.shape, jnp.float32),
-            pltpu.VMEM((2,) + probes.shape[2:], jnp.float32),
-        ],
-        compiler_params=pltpu.CompilerParams(vmem_limit_bytes=40 * 1024 * 1024),
-        name="cross",
-    )(starts, counts, object_map, change, probes, step, parts)
-
-
-def advance_kernel(parts, object_map, change, probes, step, new_map, new_probes, inbox, send, arrive):
-    row, col = (lax.axis_index("tx"), lax.axis_index("ty"))
-    peers = everyone(row, col)
-    greet(peers)
-    copies = [
-        copy_to(parts, inbox.at[k], send, arrive, k, peer) for k, peer in enumerate(peers)
-    ]
+    mine[...] = jnp.where(at == 4, cross, parts[...])
+    pl.semaphore_wait(barrier, len(peers))
+    copies = [copy_to(mine, inbox.at[k], send, arrive, k, peer) for k, peer in enumerate(peers)]
     for copy in copies:
         copy.start()
     for copy in copies:
         copy.wait()
-    modes = probes.shape[1]
-    per = modes // 2
-    total = parts[...] + jnp.sum(inbox[...], axis=0)
-    object_curve, object_slope = (total[0:1], total[1:2])
-    probe_curve, probe_slope = (total[2:3], total[3:4])
+    total = mine[...] + jnp.sum(inbox[...], axis=0)
     object_rate, probe_rate = solve_steps(
-        object_curve, total[4:5], probe_curve, object_slope, probe_slope
+        total[0:1], total[4:5], total[2:3], total[1:2], total[3:4]
     )
     object_rate = jnp.broadcast_to(object_rate, (8, parts.shape[-1]))
     probe_rate = jnp.broadcast_to(probe_rate, (8, parts.shape[-1]))
@@ -656,25 +636,28 @@
         new_probes[1, mode] = probes[1, mode] + probe_rate * step[stream, per + place]
 
 
-def advance(parts, object_map, change, probes, step):
+def advance(places, weights, object_map, change, probes, step, parts):
     return pl.pallas_call(
         advance_kernel,
         out_shape=(
             jax.ShapeDtypeStruct(object_map.shape, jnp.float32),
             jax.ShapeDtypeStruct(probes.shape, jnp.float32),
         ),
-        in_specs=[memory] * 5,
+        in_specs=[scalars, scalars] + [memory] * 5,
         out_specs=(memory, memory),
         scratch_shapes=[
+            pltpu.VMEM(object_map.shape, jnp.float32),
+            pltpu.VMEM((2,) + probes.shape[2:], jnp.float32),
+            pltpu.VMEM(parts.shape, jnp.float32),
             pltpu.VMEM((15,) + parts.shape, jnp.float32),
             pltpu.SemaphoreType.DMA((15,)),
             pltpu.SemaphoreType.DMA((15,)),
         ],
         compiler_params=pltpu.CompilerParams(
-            collective_id=2, has_side_effects=True, vmem_limit_bytes=40 * 1024 * 1024
+            collective_id=2, has_side_effects=True, vmem_limit_bytes=20 * 1024 * 1024
         ),
         name="advance",
-    )(parts, object_map, change, probes, step)
+    )(places, weights, object_map, change, probes, step, parts)
 
 
 def direct(object_field, probe_modes, positions, counts, intensity):
@@ -686,6 +669,14 @@
         [lax.axis_index("tx") * height - margin, lax.axis_index("ty") * breadth - margin]
     )
     starts = positions - anchor[None, :]
+    lanes = 2 * breadth
+    rows_at = jnp.clip(starts[:, 0], 0, height + 2 * margin - length)
+    cols_at = jnp.clip(starts[:, 1], 0, lanes - length)
+    tile = jnp.minimum(rows_at // 8, (height + 2 * margin - length) // 8 - 1)
+    shift = rows_at - 8 * tile
+    back = (lanes + margin - cols_at) % lanes
+    places = jnp.stack([tile, back, shift, (8 - shift) % 8], axis=1)
+    weights = (jnp.arange(positions.shape[0], dtype=jnp.int32) < counts[0]).astype(jnp.float32)
     object_map = widen_tiles(object_field.reshape(2, height // 8, 8, breadth))
     probes = probe_modes
     for _ in range(ITERS):
@@ -694,8 +685,7 @@
         )
         change, step, parts = combine(totals, sums)
         tiles = probes.reshape(2, modes, length // 8, 8, length)
-        parts = cross(starts, counts, object_map, change, tiles, step, parts)
-        object_map, tiles = advance(parts, object_map, change, tiles, step)
+        object_map, tiles = advance(places, weights, object_map, change, tiles, step, parts)
         probes = tiles.reshape(probes.shape)
     own = object_map[:, height // 8 : height // 4, :, :breadth]
     return (own.reshape(object_field.shape), probes)

time: 139 us -> 136 us (0.978)
  Pallas kernels: 130 us -> 126 us
    pallas_call x2, Pallas kernels: 14.2 us -> 7.86 us  [accumulate(): pl.pallas_call(functools.partial(slots_kernel, lead), out_shape=(jax.Shap...]
    pallas_call x2, Pallas kernels: 88 us -> 91.3 us  [combine(): pl.pallas_call(combine_kernel, out_shape=(jax.ShapeDtypeStruct((2, rows,...]
    pallas_call x2 -> x0, Pallas kernels: 2.71 us -> none  [cross(): pl.pallas_call(cross_kernel, out_shape=jax.ShapeDtypeStruct(parts.shape,...]
    pallas_call x2, Pallas kernels: 14.9 us -> 16.4 us  [advance(): pl.pallas_call(advance_kernel, out_shape=(jax.ShapeDtypeStruct(object_map...]
where the time goes in v3:
time: 136 us; the launch traced here: 135 us
  Pallas kernels  126 us (93%)
  local copies, waits for them, and re-layouts  7.72 us (6%)
  between operations  1.42 us (1%)
    pallas_call x2, Pallas kernels, combine(): pl.pallas_call(combine_kernel, out_shape=(jax.ShapeDtypeStruct((2, rows,...  91.3 us
    pallas_call x2, Pallas kernels, advance(): pl.pallas_call(advance_kernel, out_shape=(jax.ShapeDtypeStruct(object_map...  16.4 us
    pallas_call x1, Pallas kernels, widen_tiles(): pl.pallas_call(widen_kernel, out_shape=jax.ShapeDtypeStruct((two, 3 * hig...  10.1 us
    pallas_call x2, Pallas kernels, accumulate(): pl.pallas_call(functools.partial(slots_kernel, lead), out_shape=(jax.Shap...  7.86 us
    unnamed x20, local copies, waits for them, and re-layouts  7.08 us

profile of v3, /device:TPU:0, one launch (start us, length us, event | category | flops | bytes accessed | tf_op | source)
XLA Modules:
  0.0 134.9 jit_solution(12384026686840432110)
XLA Ops:
  1.3 0.1 pad_add_fusion.1
  1.4 0.8 copy.9
  2.1 0.1 add_select_fusion
  2.2 0.1 pad_add_fusion.places
  2.3 0.0 copy-start.8
  2.3 0.8 copy-done.8
  3.1 10.1 %widen.1.object_map = f32[2,24,8,256]{3,2,1,0:T(8,128)S(1)} custom-call(f32[2,8,8,128]{3,2,1,0:T(8,128)S(1)} %bitcast.17), custom_call_target="tpu_custom_call" | custom-call | bytes 30000000 | tf_op jit(solution)/shard_map/widen/pallas_call | solution.py:380
  13.2 0.0 copy-start
  13.2 1.2 copy-done
  14.4 0.0 copy-start.2
  14.4 1.1 copy-done.2
  15.6 0.0 copy-start.4
  15.6 1.1 copy-done.4
  16.7 0.0 copy-start.6
  16.7 1.0 copy-done.6
  17.7 3.9 %slots.2 = (f32[3,24,8,256]{3,2,1,0:T(8,128)S(1)}, f32[2,9,128,128]{3,2,1,0:T(8,128)S(1)}) custom-call(s32[6,2]{1,0:T(8,128)S(1)} %broadcast_subtract_fusion.starts, s32[1]{0:T(128)} %copy.11.counts, f32[2,24,8,256]{3,2,1,0:T(8,128)S(1)} %widen.1.object_map, f32[2,8,128,128]{3,2,1,0:T(8,128)S(1)} %copy-done, f32[6,128,128]{2,1,0:T(8,128)S(1)} %copy-done.6, ...), custom_call_target="tpu_custom_call" | custom-call | tf_op jit(solution)/shard_map/slots/pallas_call | solution.py:172
  21.6 0.0 copy-start.1
  21.6 45.3 %combine.2 = (f32[2,24,8,256]{3,2,1,0:T(8,128)S(1)}, f32[2,8,16,8,128]{4,3,2,1,0:T(8,128)S(1)}, f32[8,128]{1,0:T(8,128)S(1)}) custom-call(f32[3,24,8,256]{3,2,1,0:T(8,128)S(1)} %get-tuple-element.16.totals, f32[2,9,16,8,128]{4,3,2,1,0:T(8,128)S(1)} %bitcast.15), custom_call_target="tpu_custom_call" | custom-call | tf_op jit(solution)/shard_map/combine/pallas_call | solution.py:548
  66.9 0.0 copy-done.1
  66.9 0.0 copy-start.3
  67.0 0.0 copy-start.5
  67.0 0.0 copy-start.7
  67.0 8.7 %advance.2 = (f32[2,24,8,256]{3,2,1,0:T(8,128)S(1)}, f32[2,8,16,8,128]{4,3,2,1,0:T(8,128)S(1)}) custom-call(s32[6,4]{1,0:T(8,128)S(1)} %pad_add_fusion.places, f32[6]{0:T(128)S(1)} %compare_convert_fusion.weights, f32[2,24,8,256]{3,2,1,0:T(8,128)S(1)} %widen.1.object_map, f32[2,24,8,256]{3,2,1,0:T(8,128)S(1)} %get-tuple-element.18.change, ...), custom_call_target="tpu_custom_call" | custom-call | tf_op jit(solution)/shard_map/advance/pallas_call | solution.py:640
  75.7 0.0 copy-done.3
  75.7 0.0 copy-done.5
  75.7 0.0 copy-done.7
  75.7 3.9 %slots.3 = (f32[3,24,8,256]{3,2,1,0:T(8,128)S(1)}, f32[2,9,128,128]{3,2,1,0:T(8,128)S(1)}) custom-call(s32[6,2]{1,0:T(8,128)S(1)} %broadcast_subtract_fusion.starts, s32[1]{0:T(128)} %copy.11.counts, f32[2,24,8,256]{3,2,1,0:T(8,128)S(1)} %get-tuple-element.21.object_map, f32[2,8,128,128]{3,2,1,0:T(8,128)S(1)} %bitcast.13, f32[6,128,128]{2,1,0:T(8,128)S(1)} %copy-done.7, ...), custom_call_target="tpu_custom_call" | custom-call | tf_op jit(solution)/shard_map/slots/pallas_call | solution.py:172
  79.7 46.0 %combine.3 = (f32[2,24,8,256]{3,2,1,0:T(8,128)S(1)}, f32[2,8,16,8,128]{4,3,2,1,0:T(8,128)S(1)}, f32[8,128]{1,0:T(8,128)S(1)}) custom-call(f32[3,24,8,256]{3,2,1,0:T(8,128)S(1)} %get-tuple-element.23.totals, f32[2,9,16,8,128]{4,3,2,1,0:T(8,128)S(1)} %bitcast.14), custom_call_target="tpu_custom_call" | custom-call | tf_op jit(solution)/shard_map/combine/pallas_call | solution.py:548
  125.7 7.6 %advance.3 = (f32[2,24,8,256]{3,2,1,0:T(8,128)S(1)}, f32[2,8,16,8,128]{4,3,2,1,0:T(8,128)S(1)}) custom-call(s32[6,4]{1,0:T(8,128)S(1)} %pad_add_fusion.places, f32[6]{0:T(128)S(1)} %compare_convert_fusion.weights, f32[2,24,8,256]{3,2,1,0:T(8,128)S(1)} %get-tuple-element.21.object_map, f32[2,24,8,256]{3,2,1,0:T(8,128)S(1)} %get-tuple-element.25.change, ...), custom_call_target="tpu_custom_call" | custom-call | tf_op jit(solution)/shard_map/advance/pallas_call | solution.py:640
  133.3 0.6 slice_bitcast_fusion
  134.0 1.0 copy.12
  (2 shorter events, 0.0 us)
Async XLA Ops:
  2.3 0.8 copy-start.8
  13.2 1.2 copy-start
  14.4 1.1 copy-start.2
  15.6 1.1 copy-start.4
  16.7 1.0 copy-start.6
  21.6 45.3 %copy-start.1 = (f32[2,8,128,128]{3,2,1,0:T(8,128)S(1)}, f32[2,8,128,128]{3,2,1,0:T(8,128)}, u32[]{:S(2)}) copy-start(f32[2,8,128,128]{3,2,1,0:T(8,128)} %probes.1) | copy-start | bytes 3145732
  66.9 8.8 %copy-start.3 = (bf16[2,768,256]{2,1,0:T(8,128)(2,1)S(1)}, bf16[2,768,256]{2,1,0:T(8,128)(2,1)}, u32[]{:S(2)}) copy-start(bf16[2,768,256]{2,1,0:T(8,128)(2,1)} %constant.63.clone.rights) | copy-start | bytes 2359300
  67.0 8.8 %copy-start.5 = (bf16[2,256,768]{2,1,0:T(8,128)(2,1)S(1)}, bf16[2,256,768]{2,1,0:T(8,128)(2,1)}, u32[]{:S(2)}) copy-start(bf16[2,256,768]{2,1,0:T(8,128)(2,1)} %constant.62.clone.lefts) | copy-start | bytes 2359300
  67.0 8.8 %copy-start.7 = (f32[6,128,128]{2,1,0:T(8,128)S(1)}, f32[6,128,128]{2,1,0:T(8,128)}, u32[]{:S(2)}) copy-start(f32[6,128,128]{2,1,0:T(8,128)} %intensity.3) | copy-start | bytes 1179652

commit v4 on v3

--- a/solution.py
+++ b/solution.py
@@ -46,13 +46,7 @@
         fine = (table - coarse.astype(np.float64)).astype(ml_dtypes.bfloat16)
         return (coarse, fine)
 
-    lefts, rights = ([], [])
-    for left, right in ((forward, inverse), (inverse, forward)):
-        coarse, fine = halves(left)
-        lefts.append(np.concatenate([coarse, fine, coarse], axis=1))
-        coarse, fine = halves(right)
-        rights.append(np.concatenate([coarse, coarse, fine], axis=0))
-    return (np.stack(lefts), np.stack(rights))
+    return np.stack(halves(forward) + halves(inverse)).reshape(2, -1, 2 * length)
 
 
 def halve(value):
@@ -66,12 +60,16 @@
 
 def from_left(table, value):
     coarse, fine = halve(value)
-    return multiply(table, jnp.concatenate([coarse, coarse, fine], axis=0))
+    both = multiply(table, coarse)
+    size = value.shape[0]
+    return both[:size] + both[size:] + multiply(table[:size], fine)
 
 
 def from_right(value, table):
     coarse, fine = halve(value)
-    return multiply(jnp.concatenate([coarse, fine, coarse], axis=1), table)
+    size = value.shape[0]
+    both = multiply(jnp.concatenate([coarse, fine], axis=0), table[: value.shape[1]])
+    return both[:size] + both[size:] + multiply(coarse, table[value.shape[1] :])
 
 
 def regroup(value, length):
@@ -86,7 +84,7 @@
 
 
 def slots_kernel(
-    lead, starts, counts, object_map, probes, intensity, lefts, rights, totals, sums, window, far, lit
+    lead, starts, counts, object_map, probes, intensity, turns, totals, sums, window, far, lit
 ):
     modes, length = (probes.shape[1], probes.shape[-1])
     breadth = object_map.shape[-1]
@@ -123,8 +121,8 @@
             wave = jnp.concatenate(
                 [jnp.concatenate(waves_r, axis=1), jnp.concatenate(waves_i, axis=1)], axis=0
             )
-            half = regroup(from_left(lefts[0], wave), length)
-            spread = from_right(half, rights[0])
+            half = regroup(from_left(turns[0], wave), length)
+            spread = from_right(half, turns[1])
             far[pair] = spread
             power = spread * spread
             power = power[:, :length] + power[:, length:]
@@ -135,8 +133,8 @@
         terms_r = jnp.zeros((length, length), jnp.float32)
         terms_i = jnp.zeros((length, length), jnp.float32)
         for pair in range(modes // 2):
-            half = regroup(from_right(far[pair] * factor, rights[1]), length)
-            change = from_left(lefts[1], half)
+            half = regroup(from_right(far[pair] * factor, turns[0]), length)
+            change = from_left(turns[1], half)
             obj_r, obj_i = (window[0], window[1])
             for which in range(2):
                 mode = 2 * pair + which
@@ -167,7 +165,7 @@
     lax.fori_loop(0, counts[0], visit_slot, 0)
 
 
-def accumulate(object_map, probes, starts, counts, intensity, lefts, rights, lead):
+def accumulate(object_map, probes, starts, counts, intensity, turns, lead):
     _, modes, length, _ = probes.shape
     return pl.pallas_call(
         functools.partial(slots_kernel, lead),
@@ -175,7 +173,7 @@
             jax.ShapeDtypeStruct((3,) + object_map.shape[1:], jnp.float32),
             jax.ShapeDtypeStruct((2, modes + 1, length, length), jnp.float32),
         ),
-        in_specs=[scalars, scalars] + [memory] * 5,
+        in_specs=[scalars, scalars] + [memory] * 4,
         out_specs=(memory, memory),
         scratch_shapes=[
             pltpu.VMEM((2, length, length), jnp.float32),
@@ -184,7 +182,7 @@
         ],
         compiler_params=pltpu.CompilerParams(vmem_limit_bytes=40 * 1024 * 1024),
         name="slots",
-    )(starts, counts, object_map, probes, intensity, lefts, rights)
+    )(starts, counts, object_map, probes, intensity, turns)
 
 
 def mixing(probes, probe_step):
@@ -253,7 +251,7 @@
     margin = length // 2
     height = object_field.shape[1]
     breadth = object_field.shape[2]
-    lefts, rights = split_tables(length)
+    turns = split_tables(length)
     modes = probe_modes.shape[1]
     anchor = jnp.stack(
         [lax.axis_index("tx") * height - margin, lax.axis_index("ty") * breadth - margin]
@@ -265,7 +263,7 @@
     extended = widen(object_map, margin)
     for repeat in range(ITERS):
         tiled = extended.reshape(2, -1, 8, extended.shape[-1])
-        totals, sums = accumulate(tiled, probes, starts, counts, intensity, lefts, rights, 0)
+        totals, sums = accumulate(tiled, probes, starts, counts, intensity, turns, 0)
         totals = totals.reshape((3,) + extended.shape[1:])
         interior = fold_rims(totals, margin, height, breadth)
         change = interior[:2] / jnp.maximum(interior[2], 1.0)
@@ -664,7 +662,7 @@
     two, modes, length, _ = probe_modes.shape
     margin = length // 2
     _, height, breadth = object_field.shape
-    lefts, rights = split_tables(length)
+    turns = split_tables(length)
     anchor = jnp.stack(
         [lax.axis_index("tx") * height - margin, lax.axis_index("ty") * breadth - margin]
     )
@@ -681,7 +679,7 @@
     probes = probe_modes
     for _ in range(ITERS):
         totals, sums = accumulate(
-            object_map, probes, starts, counts, intensity, lefts, rights, margin
+            object_map, probes, starts, counts, intensity, turns, margin
         )
         change, step, parts = combine(totals, sums)
         tiles = probes.reshape(2, modes, length // 8, 8, length)

time: 136 us -> 134 us (0.985)
    pallas_call x2, Pallas kernels: 91.3 us -> 58.3 us  [combine(): pl.pallas_call(combine_kernel, out_shape=(jax.ShapeDtypeStruct((2, rows,...]
    pallas_call x2, Pallas kernels: 7.86 us -> 38.5 us  [accumulate(): pl.pallas_call(functools.partial(slots_kernel, lead), out_shape=(jax.Shap...]
    pallas_call x2, Pallas kernels: 16.4 us -> 18 us  [advance(): pl.pallas_call(advance_kernel, out_shape=(jax.ShapeDtypeStruct(object_map...]
    unnamed x20 -> x16, local copies, waits for them, and re-layouts: 7.08 us -> 5.85 us
where the time goes in v4:
time: 134 us; the launch traced here: 133 us
  Pallas kernels  125 us (93%)
  local copies, waits for them, and re-layouts  6.49 us (5%)
  between operations  1.4 us (1%)
    pallas_call x2, Pallas kernels, combine(): pl.pallas_call(combine_kernel, out_shape=(jax.ShapeDtypeStruct((2, rows,...  58.3 us
    pallas_call x2, Pallas kernels, accumulate(): pl.pallas_call(functools.partial(slots_kernel, lead), out_shape=(jax.Shap...  38.5 us
    pallas_call x2, Pallas kernels, advance(): pl.pallas_call(advance_kernel, out_shape=(jax.ShapeDtypeStruct(object_map...  18 us
    pallas_call x1, Pallas kernels, widen_tiles(): pl.pallas_call(widen_kernel, out_shape=jax.ShapeDtypeStruct((two, 3 * hig...  10.1 us
    unnamed x16, local copies, waits for them, and re-layouts  5.85 us

profile of v4, /device:TPU:0, one launch (start us, length us, event | category | flops | bytes accessed | tf_op | source)
XLA Modules:
  0.0 133.0 jit_solution(13295507551363825912)
XLA Ops:
  1.3 0.1 pad_add_fusion.1
  1.4 0.8 copy.8
  2.1 0.1 add_select_fusion
  2.2 0.1 pad_add_fusion.places
  2.3 0.0 copy-start.6
  2.3 0.8 copy-done.6
  3.1 10.1 %widen.1.object_map = f32[2,24,8,256]{3,2,1,0:T(8,128)S(1)} custom-call(f32[2,8,8,128]{3,2,1,0:T(8,128)S(1)} %bitcast.17), custom_call_target="tpu_custom_call" | custom-call | bytes 30000000 | tf_op jit(solution)/shard_map/widen/pallas_call | solution.py:378
  13.2 0.0 copy-start
  13.2 1.2 copy-done
  14.4 0.0 copy-start.2
  14.4 1.0 copy-done.2
  15.5 0.0 copy-start.4
  15.5 1.0 copy-done.4
  16.5 19.2 %slots.2 = (f32[3,24,8,256]{3,2,1,0:T(8,128)S(1)}, f32[2,9,128,128]{3,2,1,0:T(8,128)S(1)}) custom-call(s32[6,2]{1,0:T(8,128)S(1)} %broadcast_subtract_fusion.starts, s32[1]{0:T(128)} %copy.10.counts, f32[2,24,8,256]{3,2,1,0:T(8,128)S(1)} %widen.1.object_map, f32[2,8,128,128]{3,2,1,0:T(8,128)S(1)} %copy-done, f32[6,128,128]{2,1,0:T(8,128)S(1)} %copy-done.4, ...), custom_call_target="tpu_custom_call" | custom-call | tf_op jit(solution)/shard_map/slots/pallas_call | solution.py:170
  35.7 0.0 copy-start.1
  35.7 29.6 %combine.2 = (f32[2,24,8,256]{3,2,1,0:T(8,128)S(1)}, f32[2,8,16,8,128]{4,3,2,1,0:T(8,128)S(1)}, f32[8,128]{1,0:T(8,128)S(1)}) custom-call(f32[3,24,8,256]{3,2,1,0:T(8,128)S(1)} %get-tuple-element.16.totals, f32[2,9,16,8,128]{4,3,2,1,0:T(8,128)S(1)} %bitcast.15), custom_call_target="tpu_custom_call" | custom-call | tf_op jit(solution)/shard_map/combine/pallas_call | solution.py:546
  65.3 0.0 copy-done.1
  65.3 0.0 copy-start.3
  65.3 0.0 copy-start.5
  65.4 8.9 %advance.2 = (f32[2,24,8,256]{3,2,1,0:T(8,128)S(1)}, f32[2,8,16,8,128]{4,3,2,1,0:T(8,128)S(1)}) custom-call(s32[6,4]{1,0:T(8,128)S(1)} %pad_add_fusion.places, f32[6]{0:T(128)S(1)} %compare_convert_fusion.weights, f32[2,24,8,256]{3,2,1,0:T(8,128)S(1)} %widen.1.object_map, f32[2,24,8,256]{3,2,1,0:T(8,128)S(1)} %get-tuple-element.18.change, ...), custom_call_target="tpu_custom_call" | custom-call | tf_op jit(solution)/shard_map/advance/pallas_call | solution.py:638
  74.2 0.0 copy-done.3
  74.3 0.0 copy-done.5
  74.3 19.3 %slots.3 = (f32[3,24,8,256]{3,2,1,0:T(8,128)S(1)}, f32[2,9,128,128]{3,2,1,0:T(8,128)S(1)}) custom-call(s32[6,2]{1,0:T(8,128)S(1)} %broadcast_subtract_fusion.starts, s32[1]{0:T(128)} %copy.10.counts, f32[2,24,8,256]{3,2,1,0:T(8,128)S(1)} %get-tuple-element.21.object_map, f32[2,8,128,128]{3,2,1,0:T(8,128)S(1)} %bitcast.13, f32[6,128,128]{2,1,0:T(8,128)S(1)} %copy-done.5, ...), custom_call_target="tpu_custom_call" | custom-call | tf_op jit(solution)/shard_map/slots/pallas_call | solution.py:170
  93.5 28.7 %combine.3 = (f32[2,24,8,256]{3,2,1,0:T(8,128)S(1)}, f32[2,8,16,8,128]{4,3,2,1,0:T(8,128)S(1)}, f32[8,128]{1,0:T(8,128)S(1)}) custom-call(f32[3,24,8,256]{3,2,1,0:T(8,128)S(1)} %get-tuple-element.23.totals, f32[2,9,16,8,128]{4,3,2,1,0:T(8,128)S(1)} %bitcast.14), custom_call_target="tpu_custom_call" | custom-call | tf_op jit(solution)/shard_map/combine/pallas_call | solution.py:546
  122.2 9.2 %advance.3 = (f32[2,24,8,256]{3,2,1,0:T(8,128)S(1)}, f32[2,8,16,8,128]{4,3,2,1,0:T(8,128)S(1)}) custom-call(s32[6,4]{1,0:T(8,128)S(1)} %pad_add_fusion.places, f32[6]{0:T(128)S(1)} %compare_convert_fusion.weights, f32[2,24,8,256]{3,2,1,0:T(8,128)S(1)} %get-tuple-element.21.object_map, f32[2,24,8,256]{3,2,1,0:T(8,128)S(1)} %get-tuple-element.25.change, ...), custom_call_target="tpu_custom_call" | custom-call | tf_op jit(solution)/shard_map/advance/pallas_call | solution.py:638
  131.4 0.6 slice_bitcast_fusion
  132.0 1.0 copy.11
  (2 shorter events, 0.0 us)
Async XLA Ops:
  2.3 0.8 copy-start.6
  13.2 1.2 copy-start
  14.4 1.0 copy-start.2
  15.5 1.0 copy-start.4
  35.7 29.6 %copy-start.1 = (f32[2,8,128,128]{3,2,1,0:T(8,128)S(1)}, f32[2,8,128,128]{3,2,1,0:T(8,128)}, u32[]{:S(2)}) copy-start(f32[2,8,128,128]{3,2,1,0:T(8,128)} %probes.1) | copy-start | bytes 3145732
  65.3 8.9 %copy-start.3 = (bf16[2,512,256]{2,1,0:T(8,128)(2,1)S(1)}, bf16[2,512,256]{2,1,0:T(8,128)(2,1)}, u32[]{:S(2)}) copy-start(bf16[2,512,256]{2,1,0:T(8,128)(2,1)} %constant.60.clone.turns) | copy-start | bytes 1572868
  65.3 8.9 %copy-start.5 = (f32[6,128,128]{2,1,0:T(8,128)S(1)}, f32[6,128,128]{2,1,0:T(8,128)}, u32[]{:S(2)}) copy-start(f32[6,128,128]{2,1,0:T(8,128)} %intensity.3) | copy-start | bytes 1179652

commit v5 on v4

--- a/solution.py
+++ b/solution.py
@@ -523,16 +523,22 @@
         fifth.append(give(1, 8 * core + 2 * row, 2, 13 + j, along[j - 1]))
     for copy in fifth:
         copy.start()
+    early_part = give(0, 8 * core + 4 * side, 4, 17, partner)
+    early_part.start()
     parts[...] = in_rows((curve, slope, probe_curve, probe_slope), parts.shape[-1])
     halo_side.wait(send, arrive)
     wide[:, :, :, :broad] = column[...]
     wide[:, :, :, broad:] = jnp.where(early[:2], near[1], near[0])
     for copy in fifth:
         copy.wait()
-    block = got.at[:, :, pl.ds(8 * core, 8)]
-    last = copy_to(block, block, send, arrive, 17, partner)
-    last.start()
-    last.wait()
+    last = [
+        give(0, 8 * core + 4 * (1 - side), 4, 18, partner),
+        give(1, 8 * core, 8, 19, partner),
+    ]
+    for copy in last:
+        copy.start()
+    for copy in (early_part, *last):
+        copy.wait()
     step[...] = got[...]
 
 

time: 134 us -> 133 us (level)
  no operation moved by 1% of the time
where the time goes in v5:
time: 133 us
  Pallas kernels  124 us (93%)
  local copies, waits for them, and re-layouts  6.49 us (5%)
  between operations  1.4 us (1%)
    pallas_call x2, Pallas kernels, combine(): pl.pallas_call(combine_kernel, out_shape=(jax.ShapeDtypeStruct((2, rows,...  58.1 us
    pallas_call x2, Pallas kernels, accumulate(): pl.pallas_call(functools.partial(slots_kernel, lead), out_shape=(jax.Shap...  38.5 us
    pallas_call x2, Pallas kernels, advance(): pl.pallas_call(advance_kernel, out_shape=(jax.ShapeDtypeStruct(object_map...  17.7 us
    pallas_call x1, Pallas kernels, widen_tiles(): pl.pallas_call(widen_kernel, out_shape=jax.ShapeDtypeStruct((two, 3 * hig...  10.1 us
    unnamed x16, local copies, waits for them, and re-layouts  5.85 us

profile of v5, /device:TPU:0, one launch (start us, length us, event | category | flops | bytes accessed | tf_op | source)
XLA Modules:
  0.0 132.5 jit_solution(7149263332939170600)
XLA Ops:
  1.3 0.1 pad_add_fusion.1
  1.4 0.8 copy.8
  2.1 0.1 add_select_fusion
  2.2 0.1 pad_add_fusion.places
  2.3 0.0 copy-start.6
  2.3 0.8 copy-done.6
  3.1 10.1 %widen.1.object_map = f32[2,24,8,256]{3,2,1,0:T(8,128)S(1)} custom-call(f32[2,8,8,128]{3,2,1,0:T(8,128)S(1)} %bitcast.17), custom_call_target="tpu_custom_call" | custom-call | bytes 30000000 | tf_op jit(solution)/shard_map/widen/pallas_call | solution.py:378
  13.2 0.0 copy-start
  13.2 1.2 copy-done
  14.4 0.0 copy-start.2
  14.4 1.0 copy-done.2
  15.5 0.0 copy-start.4
  15.5 1.0 copy-done.4
  16.5 19.2 %slots.2 = (f32[3,24,8,256]{3,2,1,0:T(8,128)S(1)}, f32[2,9,128,128]{3,2,1,0:T(8,128)S(1)}) custom-call(s32[6,2]{1,0:T(8,128)S(1)} %broadcast_subtract_fusion.starts, s32[1]{0:T(128)} %copy.10.counts, f32[2,24,8,256]{3,2,1,0:T(8,128)S(1)} %widen.1.object_map, f32[2,8,128,128]{3,2,1,0:T(8,128)S(1)} %copy-done, f32[6,128,128]{2,1,0:T(8,128)S(1)} %copy-done.4, ...), custom_call_target="tpu_custom_call" | custom-call | tf_op jit(solution)/shard_map/slots/pallas_call | solution.py:170
  35.7 0.0 copy-start.1
  35.7 29.7 %combine.2 = (f32[2,24,8,256]{3,2,1,0:T(8,128)S(1)}, f32[2,8,16,8,128]{4,3,2,1,0:T(8,128)S(1)}, f32[8,128]{1,0:T(8,128)S(1)}) custom-call(f32[3,24,8,256]{3,2,1,0:T(8,128)S(1)} %get-tuple-element.16.totals, f32[2,9,16,8,128]{4,3,2,1,0:T(8,128)S(1)} %bitcast.15), custom_call_target="tpu_custom_call" | custom-call | tf_op jit(solution)/shard_map/combine/pallas_call | solution.py:552
  65.4 0.0 copy-done.1
  65.4 0.0 copy-start.3
  65.4 0.0 copy-start.5
  65.4 8.6 %advance.2 = (f32[2,24,8,256]{3,2,1,0:T(8,128)S(1)}, f32[2,8,16,8,128]{4,3,2,1,0:T(8,128)S(1)}) custom-call(s32[6,4]{1,0:T(8,128)S(1)} %pad_add_fusion.places, f32[6]{0:T(128)S(1)} %compare_convert_fusion.weights, f32[2,24,8,256]{3,2,1,0:T(8,128)S(1)} %widen.1.object_map, f32[2,24,8,256]{3,2,1,0:T(8,128)S(1)} %get-tuple-element.18.change, ...), custom_call_target="tpu_custom_call" | custom-call | tf_op jit(solution)/shard_map/advance/pallas_call | solution.py:644
  74.0 0.0 copy-done.3
  74.0 0.0 copy-done.5
  74.0 19.2 %slots.3 = (f32[3,24,8,256]{3,2,1,0:T(8,128)S(1)}, f32[2,9,128,128]{3,2,1,0:T(8,128)S(1)}) custom-call(s32[6,2]{1,0:T(8,128)S(1)} %broadcast_subtract_fusion.starts, s32[1]{0:T(128)} %copy.10.counts, f32[2,24,8,256]{3,2,1,0:T(8,128)S(1)} %get-tuple-element.21.object_map, f32[2,8,128,128]{3,2,1,0:T(8,128)S(1)} %bitcast.13, f32[6,128,128]{2,1,0:T(8,128)S(1)} %copy-done.5, ...), custom_call_target="tpu_custom_call" | custom-call | tf_op jit(solution)/shard_map/slots/pallas_call | solution.py:170
  93.3 28.5 %combine.3 = (f32[2,24,8,256]{3,2,1,0:T(8,128)S(1)}, f32[2,8,16,8,128]{4,3,2,1,0:T(8,128)S(1)}, f32[8,128]{1,0:T(8,128)S(1)}) custom-call(f32[3,24,8,256]{3,2,1,0:T(8,128)S(1)} %get-tuple-element.23.totals, f32[2,9,16,8,128]{4,3,2,1,0:T(8,128)S(1)} %bitcast.14), custom_call_target="tpu_custom_call" | custom-call | tf_op jit(solution)/shard_map/combine/pallas_call | solution.py:552
  121.8 9.2 %advance.3 = (f32[2,24,8,256]{3,2,1,0:T(8,128)S(1)}, f32[2,8,16,8,128]{4,3,2,1,0:T(8,128)S(1)}) custom-call(s32[6,4]{1,0:T(8,128)S(1)} %pad_add_fusion.places, f32[6]{0:T(128)S(1)} %compare_convert_fusion.weights, f32[2,24,8,256]{3,2,1,0:T(8,128)S(1)} %get-tuple-element.21.object_map, f32[2,24,8,256]{3,2,1,0:T(8,128)S(1)} %get-tuple-element.25.change, ...), custom_call_target="tpu_custom_call" | custom-call | tf_op jit(solution)/shard_map/advance/pallas_call | solution.py:644
  130.9 0.6 slice_bitcast_fusion
  131.6 1.0 copy.11
  (2 shorter events, 0.0 us)
Async XLA Ops:
  2.3 0.8 copy-start.6
  13.2 1.2 copy-start
  14.4 1.0 copy-start.2
  15.5 1.0 copy-start.4
  35.7 29.7 %copy-start.1 = (f32[2,8,128,128]{3,2,1,0:T(8,128)S(1)}, f32[2,8,128,128]{3,2,1,0:T(8,128)}, u32[]{:S(2)}) copy-start(f32[2,8,128,128]{3,2,1,0:T(8,128)} %probes.1) | copy-start | bytes 3145732
  65.4 8.6 %copy-start.3 = (bf16[2,512,256]{2,1,0:T(8,128)(2,1)S(1)}, bf16[2,512,256]{2,1,0:T(8,128)(2,1)}, u32[]{:S(2)}) copy-start(bf16[2,512,256]{2,1,0:T(8,128)(2,1)} %constant.60.clone.turns) | copy-start | bytes 1572868
  65.4 8.6 %copy-start.5 = (f32[6,128,128]{2,1,0:T(8,128)S(1)}, f32[6,128,128]{2,1,0:T(8,128)}, u32[]{:S(2)}) copy-start(f32[6,128,128]{2,1,0:T(8,128)} %intensity.3) | copy-start | bytes 1179652
